TPU v7x, 128 devices: a whole 4x4x4 slice. The times are simulated.
128 devices in a mesh: fsdp: 8 (over y_lo, z), ctx: 4 (over y_hi, core), tp: 4 (over x).
Axes of the slice: x: 4, y: 4 (y_hi: 2, y_lo: 2; y = y_hi * 2 + y_lo), z: 4, core: 2. Of those that a mesh axis runs over, the one named last changes fastest.
Arguments:
- inputs: bfloat16 [32, 1024, 960], P(('fsdp', 'tp'), 'ctx'), may hold values from -6 to 6
- seq_live: int32 [32], P(('fsdp', 'tp')), may hold values from 0 to 1, as said below
- positions: int32 [32, 1024], P(('fsdp', 'tp'), 'ctx'), may hold values from 0 to 2046, as said below
- gain_attn: bfloat16 [960], P('fsdp'), may hold values from 0.5 to 1.5
- w_query: bfloat16 [960, 960], P('fsdp'), may hold values from -0.75 to 0.75
- w_key: bfloat16 [960, 320], P('fsdp'), may hold values from -0.75 to 0.75
- w_value: bfloat16 [960, 320], P('fsdp'), may hold values from -0.1875 to 0.1875
- w_out: bfloat16 [960, 960], P('fsdp'), may hold values from -1.5 to 1.5
- gain_mlp: bfloat16 [960], P('fsdp'), may hold values from 0.5 to 1.5
- w_gate: bfloat16 [960, 2560], P('fsdp', 'tp'), may hold values from -0.1875 to 0.1875
- w_up: bfloat16 [960, 2560], P('fsdp', 'tp'), may hold values from -0.1875 to 0.1875
- w_down: bfloat16 [960, 2560], P('fsdp', 'tp'), may hold values from -0.125 to 0.125
- cotangent: float32 [32, 1024, 960], P(('fsdp', 'tp'), 'ctx'), may hold values from -6 to 6
Outputs:
- layer_out: float32 [32, 1024, 960], P(('fsdp', 'tp'), 'ctx')
- dinputs: float32 [32, 1024, 960], P(('fsdp', 'tp'), 'ctx')
- dgain_attn: float32 [960], P('fsdp')
- dw_query: float32 [960, 960], P('fsdp')
- dw_key: float32 [960, 320], P('fsdp')
- dw_value: float32 [960, 320], P('fsdp')
- dw_out: float32 [960, 960], P('fsdp')
- dgain_mlp: float32 [960], P('fsdp')
- dw_gate: float32 [960, 2560], P('fsdp', 'tp')
- dw_up: float32 [960, 2560], P('fsdp', 'tp')
- dw_down: float32 [960, 2560], P('fsdp', 'tp')
Inputs may be any that keep to these rules, and one draw needn't show every extreme that they name: `seq_live`: the slots fall into equal blocks of consecutive slots, one block for each index of fsdp; each block holds either only 1s or exactly one 0, at any slot of the block, and both kinds of block occur. `positions`: each row starts at 0 and rises by 1 or 2 from token to token; the first slot's row rises by 2 throughout.
All inputs are finite; a program needn't handle non-finite values.
Results may differ from a plain program's by a relative error of at most 0.025.
Values may be sent and summed in bfloat16 or wider, within the bound.
No kernel may reach another device: no remote copies, remote signals or barrier semaphores. Data moves between devices by JAX's collectives and lax.ppermute only.
A program may use at most 128 MiB of HBM per device.

v0:
```python
import math

import jax
import jax.numpy as jnp
from jax import lax
from jax.sharding import PartitionSpec as P

QH = 15
KVH = 5
HEAD = 64


EPSILON = 1e-05
ROPE_BASE = 100000.0


def joined_along(tiles, dim):
    tiles = jnp.moveaxis(tiles, 0, dim)
    lengths = tiles.shape
    return tiles.reshape(*lengths[:dim], lengths[dim] * lengths[dim + 1], *lengths[dim + 2 :])


def from_everyone(shard, axis):
    copies = jnp.broadcast_to(shard, (lax.axis_size(axis), *shard.shape))
    return lax.all_to_all(copies, axis, split_axis=0, concat_axis=0, tiled=True)


def collect(shard, axis, dim):
    return joined_along(from_everyone(shard, axis), dim)


def cut_along(shard, dim, devices):
    lengths = shard.shape
    tiles = shard.reshape(*lengths[:dim], devices, lengths[dim] // devices, *lengths[dim + 1 :])
    return jnp.moveaxis(tiles, dim, 0)


def sent_and_summed(shard, axis, dim):
    tiles = cut_along(shard, dim, lax.axis_size(axis))
    arrived = lax.all_to_all(tiles, axis, split_axis=0, concat_axis=0, tiled=True)
    return arrived.astype(jnp.float32).sum(axis=0)


def sum_at_owner(shard, axis, dim):
    tiles = cut_along(shard, dim, lax.axis_size(axis))
    arrived = lax.all_to_all(tiles, axis, split_axis=0, concat_axis=0, tiled=True)
    return arrived.sum(axis=0)


def sent_together(arrays, axis, dim, along):
    columns = [a.reshape(*a.shape[:along], -1) for a in arrays]
    both = jnp.concatenate(columns, axis=along)
    out, at, done = (lax.psum_scatter(both, axis, scatter_dimension=dim, tiled=True), 0, [])
    for a, column in zip(arrays, columns):
        slab = out[..., at : at + column.shape[along]]
        done.append(slab.reshape(*slab.shape[:along], *a.shape[along:]))
        at += column.shape[along]
    return tuple(done)


def over_copies(shard, axis):
    return from_everyone(shard, axis).astype(jnp.float32).sum(axis=0)


def rope_tables(position_ids):
    half_dim = HEAD // 2
    freq_index = jnp.arange(half_dim, dtype=jnp.float32)
    inverse = jnp.exp(freq_index * (-2.0 * math.log(ROPE_BASE) / HEAD))
    angles = position_ids.astype(jnp.float32)[:, None] * inverse[None, :]
    return (jnp.cos(angles)[:, None, :], jnp.sin(angles)[:, None, :])


def rotate(tensor, cos_table, sin_table):
    half_dim = tensor.shape[-1] // 2
    first_half = tensor[..., :half_dim]
    second_half = tensor[..., half_dim:]
    return jnp.concatenate(
        [
            first_half * cos_table - second_half * sin_table,
            second_half * cos_table + first_half * sin_table,
        ],
        -1,
    )


def rotate_back(tensor, cos_table, sin_table):
    half_dim = tensor.shape[-1] // 2
    first_half = tensor[..., :half_dim]
    second_half = tensor[..., half_dim:]
    return jnp.concatenate(
        [
            first_half * cos_table + second_half * sin_table,
            second_half * cos_table - first_half * sin_table,
        ],
        -1,
    )


def rms_forward(stream, gain_vector):
    scale_inv = lax.rsqrt(jnp.mean(stream * stream, -1, keepdims=True) + EPSILON)
    normed = stream * scale_inv
    return (scale_inv, normed, (normed * gain_vector.astype(jnp.float32)).astype(jnp.bfloat16))


def rms_backward(upstream, scale_inv, normed, gain_vector):
    scaled = upstream * gain_vector.astype(jnp.float32)
    inner_mean = jnp.mean(scaled * normed, -1, keepdims=True)
    return (scale_inv * (scaled - normed * inner_mean), jnp.sum(upstream * normed, 0))


def masked_scores(head_queries, head_keys, allowed, score_scale):
    scores = (
        jnp.einsum("sqgd,skd->sgqk", head_queries, head_keys, preferred_element_type=jnp.float32)
        * score_scale
    )
    return jnp.where(allowed, scores, -1e30)


def shards(
    inputs,
    seq_live,
    positions,
    gain_attn,
    w_query,
    w_key,
    w_value,
    w_out,
    gain_mlp,
    w_gate,
    w_up,
    w_down,
    cotangent,
):
    (
        full_gain_attn,
        full_gain_mlp,
        full_query,
        full_key,
        full_value,
        full_out,
        full_gate,
        full_up,
        full_down,
    ) = (
        lax.all_gather(gain_attn, "fsdp", axis=0, tiled=True),
        lax.all_gather(gain_mlp, "fsdp", axis=0, tiled=True),
        lax.all_gather(w_query, "fsdp", axis=0, tiled=True),
        lax.all_gather(w_key, "fsdp", axis=0, tiled=True),
        lax.all_gather(w_value, "fsdp", axis=0, tiled=True),
        lax.all_gather(w_out, "fsdp", axis=0, tiled=True),
        lax.all_gather(w_gate, "fsdp", axis=0, tiled=True),
        lax.all_gather(w_up, "fsdp", axis=0, tiled=True),
        lax.all_gather(w_down, "fsdp", axis=0, tiled=True),
    )
    seq_dev, local_len, model_width = inputs.shape
    full_len = local_len * lax.axis_size("ctx")
    row_count = seq_dev * local_len
    group_size = QH // KVH
    kv_dim = KVH * HEAD
    score_scale = 1.0 / math.sqrt(HEAD)
    contract_rows = (((0,), (0,)), ((), ()))
    contract_cols = (((1,), (1,)), ((), ()))
    stream = inputs.astype(jnp.float32).reshape(row_count, model_width)
    inv_one, normed_one, hidden_one = rms_forward(stream, full_gain_attn)
    cos_table, sin_table = rope_tables(positions.reshape(row_count))
    query_lin = jnp.dot(hidden_one, full_query, preferred_element_type=jnp.float32).reshape(
        row_count, QH, HEAD
    )
    queries = rotate(query_lin, cos_table, sin_table).astype(jnp.bfloat16)
    key_lin = jnp.dot(hidden_one, full_key, preferred_element_type=jnp.float32).reshape(
        row_count, KVH, HEAD
    )
    key_rows = rotate(key_lin, cos_table, sin_table).astype(jnp.bfloat16)
    value_rows = jnp.dot(hidden_one, full_value, preferred_element_type=jnp.float32).astype(
        jnp.bfloat16
    )
    packed = jnp.concatenate([key_rows.reshape(row_count, kv_dim), value_rows], 1).reshape(
        seq_dev, local_len, 2 * kv_dim
    )
    gathered = collect(packed, "ctx", 1)
    all_keys = gathered[..., :kv_dim].reshape(seq_dev, full_len, KVH, HEAD)
    all_values = gathered[..., kv_dim:].reshape(seq_dev, full_len, KVH, HEAD)
    query_groups = queries.reshape(seq_dev, local_len, KVH, group_size, HEAD)
    query_index = lax.axis_index("ctx") * local_len + jnp.arange(local_len, dtype=jnp.int32)
    allowed = query_index[:, None] >= jnp.arange(full_len, dtype=jnp.int32)[None, :]
    log_totals = []
    attended_parts = []
    for head_index in range(KVH):
        scores = masked_scores(
            query_groups[:, :, head_index], all_keys[:, :, head_index], allowed, score_scale
        )
        row_top = jnp.max(scores, -1, keepdims=True)
        log_total = row_top + jnp.log(jnp.sum(jnp.exp(scores - row_top), -1, keepdims=True))
        probs_b = jnp.exp(scores - log_total).astype(jnp.bfloat16)
        attended_parts.append(
            jnp.einsum(
                "sgqk,skd->sqgd",
                probs_b,
                all_values[:, :, head_index],
                preferred_element_type=jnp.float32,
            )
        )
        log_totals.append(log_total)
    attended = jnp.stack(attended_parts, 2).astype(jnp.bfloat16).reshape(row_count, QH * HEAD)
    mid_stream = stream + jnp.dot(attended, full_out, preferred_element_type=jnp.float32)
    inv_two, normed_two, hidden_two = rms_forward(mid_stream, full_gain_mlp)
    mlp_input = collect(hidden_two.reshape(seq_dev, local_len, model_width), "tp", 0).reshape(
        -1, model_width
    )
    gate_pre = jnp.dot(mlp_input, full_gate, preferred_element_type=jnp.float32)
    up_pre = jnp.dot(mlp_input, full_up, preferred_element_type=jnp.float32)
    sigmoid_gate = jax.nn.sigmoid(gate_pre)
    activated = (gate_pre * sigmoid_gate * up_pre).astype(jnp.bfloat16)
    partial_out = lax.dot_general(
        activated, full_down, contract_cols, preferred_element_type=jnp.float32
    )
    mlp_out = sent_and_summed(
        partial_out.reshape(-1, local_len, model_width).astype(jnp.bfloat16), "tp", 0
    ).reshape(row_count, model_width)
    layer_out = mid_stream + mlp_out
    upstream = (cotangent * seq_live.astype(jnp.float32)[:, None, None]).reshape(
        row_count, model_width
    )
    upstream_b = upstream.astype(jnp.bfloat16)
    grad_rows = collect(upstream_b.reshape(seq_dev, local_len, model_width), "tp", 0).reshape(
        -1, model_width
    )
    grad_act = jnp.dot(grad_rows, full_down, preferred_element_type=jnp.float32)
    up_back = (grad_act * gate_pre * sigmoid_gate).astype(jnp.bfloat16)
    gate_back = (grad_act * up_pre * sigmoid_gate * (1.0 + gate_pre * (1.0 - sigmoid_gate))).astype(
        jnp.bfloat16
    )
    grad_down_full = lax.dot_general(
        grad_rows, activated, contract_rows, preferred_element_type=jnp.float32
    )
    grad_gate_full = lax.dot_general(
        mlp_input, gate_back, contract_rows, preferred_element_type=jnp.float32
    )
    grad_up_full = lax.dot_general(
        mlp_input, up_back, contract_rows, preferred_element_type=jnp.float32
    )
    partial_in = lax.dot_general(
        gate_back, full_gate, contract_cols, preferred_element_type=jnp.float32
    ) + lax.dot_general(up_back, full_up, contract_cols, preferred_element_type=jnp.float32)
    grad_hidden_two = sum_at_owner(partial_in.reshape(-1, local_len, model_width), "tp", 0).reshape(
        row_count, model_width
    )
    back_two, grad_gain_two = rms_backward(grad_hidden_two, inv_two, normed_two, full_gain_mlp)
    grad_mid = upstream + back_two
    grad_mid_b = grad_mid.astype(jnp.bfloat16)
    grad_out_full = lax.dot_general(
        attended, grad_mid_b, contract_rows, preferred_element_type=jnp.float32
    )
    grad_attended = lax.dot_general(
        grad_mid_b, full_out, contract_cols, preferred_element_type=jnp.float32
    ).astype(jnp.bfloat16)
    grad_attended = grad_attended.reshape(seq_dev, local_len, KVH, group_size, HEAD)
    key_grad_parts = []
    value_grad_parts = []
    query_grad_parts = []
    for head_index in range(KVH):
        head_queries = query_groups[:, :, head_index]
        head_keys = all_keys[:, :, head_index]
        head_values = all_values[:, :, head_index]
        head_grads = grad_attended[:, :, head_index]
        scores = masked_scores(head_queries, head_keys, allowed, score_scale)
        softmax = jnp.exp(scores - log_totals[head_index])
        probs_b = softmax.astype(jnp.bfloat16)
        grad_probs = jnp.einsum(
            "sqgd,skd->sgqk", head_grads, head_values, preferred_element_type=jnp.float32
        )
        row_inner = jnp.sum(softmax * grad_probs, -1, keepdims=True)
        grad_scores = (softmax * (grad_probs - row_inner) * score_scale).astype(jnp.bfloat16)
        value_grad_parts.append(
            jnp.einsum("sgqk,sqgd->skd", probs_b, head_grads, preferred_element_type=jnp.float32)
        )
        key_grad_parts.append(
            jnp.einsum(
                "sgqk,sqgd->skd", grad_scores, head_queries, preferred_element_type=jnp.float32
            )
        )
        query_grad_parts.append(
            jnp.einsum("sgqk,skd->sqgd", grad_scores, head_keys, preferred_element_type=jnp.float32)
        )
    grad_keys_all = jnp.stack(key_grad_parts, 2).reshape(seq_dev, full_len, kv_dim)
    grad_values_all = jnp.stack(value_grad_parts, 2).reshape(seq_dev, full_len, kv_dim)
    grad_queries = jnp.stack(query_grad_parts, 2).reshape(row_count, QH, HEAD)
    packed_grads = jnp.concatenate([grad_keys_all, grad_values_all], -1)
    own_grads = sum_at_owner(packed_grads, "ctx", 1).reshape(row_count, 2 * kv_dim)
    grad_key_lin = (
        rotate_back(own_grads[:, :kv_dim].reshape(row_count, KVH, HEAD), cos_table, sin_table)
        .astype(jnp.bfloat16)
        .reshape(row_count, kv_dim)
    )
    grad_value_lin = own_grads[:, kv_dim:].astype(jnp.bfloat16)
    grad_query_lin = (
        rotate_back(grad_queries, cos_table, sin_table)
        .astype(jnp.bfloat16)
        .reshape(row_count, QH * HEAD)
    )
    grad_query_full = lax.dot_general(
        hidden_one, grad_query_lin, contract_rows, preferred_element_type=jnp.float32
    )
    grad_key_full = lax.dot_general(
        hidden_one, grad_key_lin, contract_rows, preferred_element_type=jnp.float32
    )
    grad_value_full = lax.dot_general(
        hidden_one, grad_value_lin, contract_rows, preferred_element_type=jnp.float32
    )
    grad_hidden_one = lax.dot_general(
        grad_query_lin, full_query, contract_cols, preferred_element_type=jnp.float32
    )
    grad_hidden_one = grad_hidden_one + lax.dot_general(
        grad_key_lin, full_key, contract_cols, preferred_element_type=jnp.float32
    )
    grad_hidden_one = grad_hidden_one + lax.dot_general(
        grad_value_lin, full_value, contract_cols, preferred_element_type=jnp.float32
    )
    back_one, grad_gain_one = rms_backward(grad_hidden_one, inv_one, normed_one, full_gain_attn)
    grad_input = grad_mid + back_one
    (
        share_gain_one,
        share_gain_two,
        share_query,
        share_key,
        share_value,
        share_out,
        share_gate,
        share_up,
        share_down,
    ) = (
        lax.psum_scatter(
            grad_gain_one.astype(jnp.bfloat16), "fsdp", scatter_dimension=0, tiled=True
        ).astype(jnp.float32),
        *tuple(
            (
                part.astype(jnp.float32)
                for part in sent_together(
                    (
                        grad_gain_two.astype(jnp.bfloat16),
                        grad_query_full.astype(jnp.bfloat16),
                        grad_key_full.astype(jnp.bfloat16),
                        grad_value_full.astype(jnp.bfloat16),
                        grad_out_full.astype(jnp.bfloat16),
                        grad_gate_full.astype(jnp.bfloat16),
                        grad_up_full.astype(jnp.bfloat16),
                        grad_down_full.astype(jnp.bfloat16),
                    ),
                    "fsdp",
                    0,
                    1,
                )
            )
        ),
    )
    share_gate, share_up, share_down = (
        over_copies(share_gate.astype(jnp.bfloat16), "ctx").astype(jnp.float32),
        over_copies(share_up.astype(jnp.bfloat16), "ctx").astype(jnp.float32),
        over_copies(share_down.astype(jnp.bfloat16), "ctx").astype(jnp.float32),
    )
    share_gain_one, share_gain_two, share_query, share_key, share_value, share_out = (
        lax.psum(share_gain_one.astype(jnp.bfloat16), ("ctx", "tp")).astype(jnp.float32),
        lax.psum(share_gain_two.astype(jnp.bfloat16), ("ctx", "tp")).astype(jnp.float32),
        lax.psum(share_query.astype(jnp.bfloat16), ("ctx", "tp")).astype(jnp.float32),
        lax.psum(share_key.astype(jnp.bfloat16), ("ctx", "tp")).astype(jnp.float32),
        lax.psum(share_value.astype(jnp.bfloat16), ("ctx", "tp")).astype(jnp.float32),
        lax.psum(share_out.astype(jnp.bfloat16), ("ctx", "tp")).astype(jnp.float32),
    )
    return (
        layer_out.reshape(seq_dev, local_len, model_width),
        grad_input.reshape(seq_dev, local_len, model_width),
        share_gain_one,
        share_query,
        share_key,
        share_value,
        share_out,
        share_gain_two,
        share_gate,
        share_up,
        share_down,
    )


def solution(mesh):
    placed = (
        P(("fsdp", "tp"), "ctx", None),
        P(("fsdp", "tp")),
        P(("fsdp", "tp"), "ctx"),
        P("fsdp"),
        P("fsdp", None),
        P("fsdp", None),
        P("fsdp", None),
        P("fsdp", None),
        P("fsdp"),
        P("fsdp", "tp"),
        P("fsdp", "tp"),
        P("fsdp", "tp"),
        P(("fsdp", "tp"), "ctx", None),
    )
    return jax.shard_map(
        shards,
        mesh=mesh,
        in_specs=placed,
        out_specs=(
            P(("fsdp", "tp"), "ctx", None),
            P(("fsdp", "tp"), "ctx", None),
            P("fsdp"),
            P("fsdp", None),
            P("fsdp", None),
            P("fsdp", None),
            P("fsdp", None),
            P("fsdp"),
            P("fsdp", "tp"),
            P("fsdp", "tp"),
            P("fsdp", "tp"),
        ),
        check_vma=False,
    )
```

profile of v0, /device:TPU:1, one launch (start us, length us, event | category | flops | bytes accessed | tf_op | source)
XLA Modules:
  0.0 706.8 jit_solution(10042288850751372710)
XLA Ops:
  9.4 28.6 %all-gather = bf16[8,120,320]{1,2,0:T(8,128)(2,1)S(1)} all-gather(bf16[1,120,320]{1,2,0:T(8,128)(2,1)} %bitcast.612), channel_id=1, replica_groups=mesh['fsdp'=8,'ctx'=4,'tp'=4] {'fsdp'}, dimensions={0}, use_global_device_ids=true | all-gather | bytes 691200 | tf_op jit(solution)/shard_map/all_gather | solution.py:148
  38.0 26.0 %all-gather.1 = bf16[8,120,320]{1,2,0:T(8,128)(2,1)S(1)} all-gather(bf16[1,120,320]{1,2,0:T(8,128)(2,1)} %bitcast.613), channel_id=1, replica_groups=mesh['fsdp'=8,'ctx'=4,'tp'=4] {'fsdp'}, dimensions={0}, use_global_device_ids=true | all-gather | bytes 691200 | tf_op jit(solution)/shard_map/all_gather | solution.py:149
  68.3 16.4 %all-reduce.5 = (bf16[960]{0:T(1024)(128)(2,1)S(1)}, bf16[960]{0:T(1024)(128)(2,1)S(1)}) all-reduce(bf16[960]{0:T(1024)(128)(2,1)S(1)} %dynamic-update-slice, bf16[960]{0:T(1024)(128)(2,1)S(1)} %dynamic-update-slice.1), channel_id=1, replica_groups=mesh['fsdp'=8,'ctx'=4,'tp'=4] {'fsdp'}, use_global_device_ids=true, to_apply=%add | all-reduce | flops 1920 | bytes 7680
  89.3 16.3 %all-to-all-start = ((bf16[4,1,256,640]{2,3,1,0:T(8,128)(2,1)}), bf16[4,1,256,640]{2,3,1,0:T(8,128)(2,1)S(1)}, u32[]{:S(2)}, u32[]{:S(2)}) async-start(bf16[4,1,256,640]{2,3,1,0:T(8,128)(2,1)} %broadcast_in_dim.38), calls=%async_computation | async-start | bytes 2621440 | tf_op jit(solution)/shard_map/all_to_all | solution.py:25
  107.9 23.7 %all-to-all-done = bf16[4,1,256,640]{2,3,1,0:T(8,128)(2,1)S(1)} async-done(((bf16[4,1,256,640]{2,3,1,0:T(8,128)(2,1)}), bf16[4,1,256,640]{2,3,1,0:T(8,128)(2,1)S(1)}, u32[]{:S(2)}, u32[]{:S(2)}) %all-to-all-start) | async-done | bytes 1310752 | tf_op jit(solution)/shard_map/all_to_all | solution.py:25
  131.6 2.4 broadcast_in_dim.78
  134.0 4.8 all-to-all-start.3
  140.8 2.3 copy.190
  143.4 3.1 copy.192
  148.2 2.2 fusion.128
  161.9 2.7 multiply_reduce_fusion.2
  166.6 2.4 broadcast_in_dim.77
  169.0 4.4 all-to-all-start.1
  174.1 3.1 copy.200
  178.9 17.2 %all-to-all-done.1 = bf16[4,1,256,960]{2,3,1,0:T(8,128)(2,1)} async-done(((bf16[4,1,256,960]{2,3,1,0:T(8,128)(2,1)}), bf16[4,1,256,960]{2,3,1,0:T(8,128)(2,1)}, u32[]{:S(2)}, u32[]{:S(2)}) %all-to-all-start.1) | async-done | bytes 1966112 | tf_op jit(solution)/shard_map/all_to_all | solution.py:25
  196.1 3.1 copy.198
  200.9 5.3 fusion.133
  206.2 5.2 fusion.132
  211.4 3.9 all-gather.16.cloned.1.call-done
  215.3 7.8 %multiply_convert_fusion = (bf16[1024,640]{1,0:T(8,128)(2,1)}, bf16[1024,640]{1,0:T(8,128)(2,1)}, bf16[1024,640]{1,0:T(8,128)(2,1)S(1)}) fusion(f32[1024,640]{1,0:T(8,128)} %fusion.132, f32[1024,640]{1,0:T(8,128)} %fusion.133, bf16[1024,960]{0,1:T(8,128)(2,1)} %bitcast.598, bf16[960,640]{1,0:T(8,128)(2,1)} %all-gather.16.cloned.1.call-done), kind=kOutput, calls=%fused_computation.47 | convolution fusion | flops 1268776960 | bytes 12369920 | tf_op jit(solution)/shard_map/dot_general | solution.py:228
  224.2 3.0 convolution_convert_fusion.2
  227.2 4.7 convert_element_type.260
  231.9 3.1 copy.199
  234.9 4.5 all-to-all-start.2
  239.4 3.6 fusion.134
  243.0 3.6 convolution_add_fusion
  246.6 5.4 reshape_reshape.11
  252.0 4.7 copy.201
  258.5 5.0 all-to-all-start.4
  263.5 4.8 convolution_convert_fusion.3
  268.3 2.7 convolution_convert_fusion.4
  271.0 2.8 convolution_convert_fusion.5
  273.8 2.9 convert_reduce_fusion
  276.7 25.9 %all-to-all-done.4 = f32[4,1,256,960]{2,3,1,0:T(8,128)} async-done(((f32[4,1,256,960]{2,3,1,0:T(8,128)}), f32[4,1,256,960]{2,3,1,0:T(8,128)}, u32[]{:S(2)}, u32[]{:S(2)}) %all-to-all-start.4) | async-done | bytes 3932192 | tf_op jit(solution)/shard_map/all_to_all | solution.py:46
  302.5 3.4 reduce_sum.206
  306.0 2.0 multiply_reduce_fusion
  308.1 2.9 bitcast_add_fusion
  314.6 2.3 fusion
  317.2 2.2 fusion.4
  319.8 2.3 fusion.8
  322.1 2.2 fusion.12
  335.5 2.8 concatenate.49
  338.3 2.7 copy.218
  340.9 3.7 fusion.34
  361.7 12.4 %all-to-all-start.5 = ((f32[4,1,256,640]{2,3,1,0:T(8,128)}), f32[4,1,256,640]{2,3,1,0:T(8,128)}, u32[]{:S(2)}, u32[]{:S(2)}) async-start(f32[4,1,256,640]{2,3,1,0:T(8,128)} %pad_maximum_fusion), calls=%async_computation.5 | async-start | bytes 5242880 | tf_op jit(solution)/shard_map/all_to_all | solution.py:46
  374.1 2.7 fusion.54
  385.7 3.0 convolution_convert_fusion
  388.7 17.3 %all-to-all-done.5 = f32[4,1,256,640]{2,3,1,0:T(8,128)} async-done(((f32[4,1,256,640]{2,3,1,0:T(8,128)}), f32[4,1,256,640]{2,3,1,0:T(8,128)}, u32[]{:S(2)}, u32[]{:S(2)}) %all-to-all-start.5) | async-done | bytes 2621472 | tf_op jit(solution)/shard_map/all_to_all | solution.py:46
  406.0 2.8 reduce_sum.213
  409.8 2.3 convolution_convert_fusion.6
  412.8 2.3 copy.221
  418.0 2.2 copy.220
  420.3 16.4 %concatenate.52 = bf16[960,4481]{1,0:T(8,128)(2,1)} concatenate(bf16[960,1]{1,0:T(8,128)(2,1)} %convert_element_type.296, bf16[960,960]{1,0:T(8,128)(2,1)S(1)} %convolution_convert_fusion.1, bf16[960,320]{1,0:T(8,128)(2,1)} %copy.220, bf16[960,320]{1,0:T(8,128)(2,1)} %copy.221, bf16[960,960]{1,0:T(8,128)(2,1)} %convolution_convert_fusion, ...), dimensions={1} | concatenate | bytes 17207040 | tf_op jit(solution)/shard_map/concatenate | solution.py:52
  441.4 88.8 %reduce-scatter.2.cloned.1.call-done = bf16[120,4481]{1,0:T(8,128)(2,1)} async-done(((bf16[960,4481]{1,0:T(8,128)(2,1)}), bf16[120,4481]{1,0:T(8,128)(2,1)}) %reduce-scatter.2.cloned.1.call-update) | async-done | bytes 1075456 | tf_op jit(solution)/shard_map/reduce_scatter | solution.py:53
  532.4 4.9 all-to-all-start.8
  537.3 2.1 fusion.72
  539.4 8.3 %all-to-all-done.8 = bf16[4,120,640]{2,1,0:T(8,128)(2,1)} async-done(((bf16[4,120,640]{2,1,0:T(8,128)(2,1)}), bf16[4,120,640]{2,1,0:T(8,128)(2,1)}, u32[]{:S(2)}, u32[]{:S(2)}) %all-to-all-start.8) | async-done | bytes 614432 | tf_op jit(solution)/shard_map/all_to_all | solution.py:25
  548.6 4.4 all-to-all-start.7
  554.8 2.0 fusion.124
  556.8 6.5 all-to-all-done.7
  564.2 5.1 all-to-all-start.6
  570.5 17.2 %all-reduce.2 = bf16[960]{0:T(1024)(128)(2,1)S(1)} all-reduce(bf16[960]{0:T(1024)(128)(2,1)S(1)} %get-tuple-element.79), channel_id=2, replica_groups=mesh['fsdp'=8,'ctx'=4,'tp'=4] {'fsdp'}, use_global_device_ids=true, to_apply=%region_23.24.clone | all-reduce | flops 960 | bytes 3840
  588.6 32.8 %all-reduce.3 = (bf16[120]{0:T(256)(128)(2,1)S(1)}, bf16[120]{0:T(256)(128)(2,1)S(1)}) all-reduce(bf16[120]{0:T(256)(128)(2,1)S(1)} %dynamic-slice.3, bf16[120]{0:T(256)(128)(2,1)S(1)} %slice_reduce_fusion), channel_id=1, replica_groups=mesh['fsdp'=8,'ctx'=4,'tp'=4] {'ctx','tp'}, use_global_device_ids=true, to_apply=%region_24.25 | all-reduce | flops 240 | bytes 960 | tf_op jit(solution)/shard_map/psum | solution.py:362
  627.1 65.7 %all-reduce.8.cloned.1.call-done = (bf16[120,320]{1,0:T(8,128)(2,1)}, bf16[120,320]{1,0:T(8,128)(2,1)}, bf16[120,960]{1,0:T(8,128)(2,1)}, bf16[120,960]{1,0:T(8,128)(2,1)}) async-done(((bf16[120,320]{1,0:T(8,128)(2,1)}, bf16[120,320]{1,0:T(8,128)(2,1)}, bf16[120,960]{1,0:T(8,128)(2,1)}, bf16[120,960]{1,0:T(8,128)(2,1)}), (bf16[120,320]{1,0:T(8,128)(2,1)}, bf16[120,320]{1,0:T(8,128)(2,1)}, ...) | async-done | bytes 614416 | tf_op jit(solution)/shard_map/psum | solution.py:365
  (239 shorter events, 106.3 us)
Async XLA Ops:
  7.2 136.2 %all-gather.8.cloned.1.call-start = ((), (), s32[]{:S(2)}) async-start(), calls=%async_computation.10 | async-start | bytes 2211840 | tf_op jit(solution)/shard_map/all_gather | solution.py:147
  7.9 154.0 %all-gather.10.cloned.1.call-start = ((), (), s32[]{:S(2)}) async-start(), calls=%async_computation.11 | async-start | bytes 2211840 | tf_op jit(solution)/shard_map/all_gather | solution.py:150
  8.7 192.2 %all-gather.14.cloned.1.call-start = ((), (), s32[]{:S(2)}) async-start(), calls=%async_computation.13 | async-start | bytes 1382400 | tf_op jit(solution)/shard_map/all_gather | solution.py:152
  84.7 2.0 copy-start.25
  85.7 1.9 copy-start.42
  88.1 18.9 %copy-start.38 = (f32[1,256,960]{1,2,0:T(8,128)S(1)}, f32[1,256,960]{1,2,0:T(8,128)}, u32[]{:S(2)}) copy-start(f32[1,256,960]{1,2,0:T(8,128)} %param.25) | copy-start | bytes 2949124
  89.3 42.3 %all-to-all-start = ((bf16[4,1,256,640]{2,3,1,0:T(8,128)(2,1)}), bf16[4,1,256,640]{2,3,1,0:T(8,128)(2,1)S(1)}, u32[]{:S(2)}, u32[]{:S(2)}) async-start(bf16[4,1,256,640]{2,3,1,0:T(8,128)(2,1)} %broadcast_in_dim.38), calls=%async_computation | async-start | bytes 2621440 | tf_op jit(solution)/shard_map/all_to_all | solution.py:25
  105.6 100.6 %all-gather.12.cloned.1.call-start = ((), (), s32[]{:S(2)}) async-start(), calls=%async_computation.12 | async-start | bytes 1382400 | tf_op jit(solution)/shard_map/all_gather | solution.py:151
  107.0 40.5 %copy-start.30 = (pred[256,1024]{0,1:T(8,128)(4,1)}, pred[256,1024]{0,1:T(8,128)(4,1)S(1)}, u32[]{:S(2)}) copy-start(pred[256,1024]{0,1:T(8,128)(4,1)S(1)} %iota_compare_fusion) | copy-start | bytes 786436
  134.0 32.6 %all-to-all-start.3 = ((bf16[4,1,256,960]{2,3,1,0:T(8,128)(2,1)}), bf16[4,1,256,960]{2,3,1,0:T(8,128)(2,1)}, u32[]{:S(2)}, u32[]{:S(2)}) async-start(bf16[4,1,256,960]{2,3,1,0:T(8,128)(2,1)} %broadcast_in_dim.78), calls=%async_computation.3 | async-start | bytes 3932160 | tf_op jit(solution)/shard_map/all_to_all | solution.py:25
  143.4 4.1 copy-start.35
  147.4 3.9 copy-start.10
  147.4 4.6 copy-start.51
  148.2 5.9 copy-start.6
  148.2 2.2 copy-start.31
  148.2 2.3 copy-start.36
  151.3 6.9 copy-start
  152.0 7.4 %copy-start.3 = (f32[1,3,256,1024]{2,3,1,0:T(8,128)}, f32[1,3,256,1024]{2,3,1,0:T(8,128)S(1)}, u32[]{:S(2)}) copy-start(f32[1,3,256,1024]{2,3,1,0:T(8,128)S(1)} %get-tuple-element.122) | copy-start | bytes 9437188
  152.8 7.9 %copy-start.8 = (f32[1,3,256,1024]{2,3,1,0:T(8,128)}, f32[1,3,256,1024]{2,3,1,0:T(8,128)S(1)}, u32[]{:S(2)}) copy-start(f32[1,3,256,1024]{2,3,1,0:T(8,128)S(1)} %get-tuple-element.124) | copy-start | bytes 9437188
  169.0 27.1 %all-to-all-start.1 = ((bf16[4,1,256,960]{2,3,1,0:T(8,128)(2,1)}), bf16[4,1,256,960]{2,3,1,0:T(8,128)(2,1)}, u32[]{:S(2)}, u32[]{:S(2)}) async-start(bf16[4,1,256,960]{2,3,1,0:T(8,128)(2,1)} %broadcast_in_dim.77), calls=%async_computation.1 | async-start | bytes 3932160 | tf_op jit(solution)/shard_map/all_to_all | solution.py:25
  173.5 41.8 %all-gather.16.cloned.1.call-start = ((), (), s32[]{:S(2)}) async-start(), calls=%async_computation.14 | async-start | bytes 1382400 | tf_op jit(solution)/shard_map/all_gather | solution.py:153
  215.3 8.9 %copy-start.53 = (bf16[960,640]{1,0:T(8,128)(2,1)S(1)}, bf16[960,640]{1,0:T(8,128)(2,1)}, u32[]{:S(2)}) copy-start(bf16[960,640]{1,0:T(8,128)(2,1)} %all-gather.16.cloned.1.call-done) | copy-start | bytes 3686404
  234.9 23.5 %all-to-all-start.2 = ((bf16[4,1,256,960]{2,3,1,0:T(8,128)(2,1)}), bf16[4,1,256,960]{2,3,1,0:T(8,128)(2,1)}, u32[]{:S(2)}, u32[]{:S(2)}) async-start(bf16[4,1,256,960]{2,3,1,0:T(8,128)(2,1)} %copy.199), calls=%async_computation.2 | async-start | bytes 3932160 | tf_op jit(solution)/shard_map/all_to_all | solution.py:40
  239.4 3.6 copy-start.39
  239.4 3.6 copy-start.48
  258.5 44.1 %all-to-all-start.4 = ((f32[4,1,256,960]{2,3,1,0:T(8,128)}), f32[4,1,256,960]{2,3,1,0:T(8,128)}, u32[]{:S(2)}, u32[]{:S(2)}) async-start(f32[4,1,256,960]{2,3,1,0:T(8,128)} %copy.201), calls=%async_computation.4 | async-start | bytes 7864320 | tf_op jit(solution)/shard_map/all_to_all | solution.py:46
  263.4 4.8 copy-start.40
  263.5 4.8 copy-start.46
  268.3 2.7 copy-start.54
  306.0 2.1 copy-start.27
  306.0 2.1 copy-start.29
  308.1 2.9 copy-start.45
  311.0 2.2 copy-start.7
  311.0 3.6 copy-start.9
  311.0 3.6 copy-start.33
  314.6 2.6 copy-start.4
  317.2 2.6 copy-start.1
  325.1 2.7 copy-start.11
  340.9 3.7 copy-start.5
  340.9 4.7 copy-start.24
  344.6 11.8 %copy-start.20 = (bf16[3,256,1024]{1,2,0:T(8,128)(2,1)}, bf16[3,256,1024]{1,2,0:T(8,128)(2,1)S(1)}, u32[]{:S(2)}) copy-start(bf16[3,256,1024]{1,2,0:T(8,128)(2,1)S(1)} %fusion.34) | copy-start | bytes 4718596
  345.7 2.4 copy-start.2
  345.7 3.4 copy-start.23
  346.4 8.7 %copy-start.15 = (bf16[3,256,1024]{1,2,0:T(8,128)(2,1)}, bf16[3,256,1024]{1,2,0:T(8,128)(2,1)S(1)}, u32[]{:S(2)}) copy-start(bf16[3,256,1024]{1,2,0:T(8,128)(2,1)S(1)} %fusion.33) | copy-start | bytes 4718596
  349.1 2.4 copy-start.22
  349.8 4.0 copy-start.17
  352.5 3.9 copy-start.19
  353.8 2.6 copy-start.52
  357.7 2.2 copy-start.34
  361.7 15.1 %copy-start.18 = (bf16[3,256,1024]{1,2,0:T(8,128)(2,1)S(1)}, bf16[3,256,1024]{1,2,0:T(8,128)(2,1)}, u32[]{:S(2)}) copy-start(bf16[3,256,1024]{1,2,0:T(8,128)(2,1)} %copy-done.17) | copy-start | bytes 4718596
  361.7 44.3 %all-to-all-start.5 = ((f32[4,1,256,640]{2,3,1,0:T(8,128)}), f32[4,1,256,640]{2,3,1,0:T(8,128)}, u32[]{:S(2)}, u32[]{:S(2)}) async-start(f32[4,1,256,640]{2,3,1,0:T(8,128)} %pad_maximum_fusion), calls=%async_computation.5 | async-start | bytes 5242880 | tf_op jit(solution)/shard_map/all_to_all | solution.py:46
  374.1 4.7 copy-start.16
  374.1 156.1 %reduce-scatter.2.cloned.1.call-start = ((), (), s32[]{:S(2)}) async-start(), calls=%async_computation.15 | async-start | bytes 9953280 | tf_op jit(solution)/shard_map/reduce_scatter | solution.py:53
  374.1 6.7 copy-start.21
  380.7 4.3 copy-start.26
  382.8 3.0 copy-start.14
  436.6 1.6 copy-start.44
  438.2 1.8 copy-start.43
  438.2 1.8 copy-start.50
  440.0 97.3 %copy-start.37 = (f32[256,640]{0,1:T(8,128)S(1)}, f32[256,640]{0,1:T(8,128)}, u32[]{:S(2)}) copy-start(f32[256,640]{0,1:T(8,128)} %reduce_sum.213) | copy-start | bytes 1966084
  532.4 15.3 %all-to-all-start.8 = ((bf16[4,120,640]{2,1,0:T(8,128)(2,1)}), bf16[4,120,640]{2,1,0:T(8,128)(2,1)}, u32[]{:S(2)}, u32[]{:S(2)}) async-start(bf16[4,120,640]{2,1,0:T(8,128)(2,1)} %broadcast_in_dim.81), calls=%async_computation.9 | async-start | bytes 1228800 | tf_op jit(solution)/shard_map/all_to_all | solution.py:25
  548.6 14.7 %all-to-all-start.7 = ((bf16[4,120,640]{2,1,0:T(8,128)(2,1)}), bf16[4,120,640]{2,1,0:T(8,128)(2,1)S(1)}, u32[]{:S(2)}, u32[]{:S(2)}) async-start(bf16[4,120,640]{2,1,0:T(8,128)(2,1)} %broadcast_in_dim.80), calls=%async_computation.8 | async-start | bytes 1228800 | tf_op jit(solution)/shard_map/all_to_all | solution.py:25
  553.0 139.8 %all-reduce.8.cloned.1.call-start = ((), (), s32[]{:S(2)}) async-start(), calls=%async_computation.16 | async-start | bytes 1351680 | tf_op jit(solution)/shard_map/psum | solution.py:365
  564.2 61.0 %all-to-all-start.6 = ((bf16[4,120,640]{2,1,0:T(8,128)(2,1)}), bf16[4,120,640]{2,1,0:T(8,128)(2,1)}, u32[]{:S(2)}, u32[]{:S(2)}) async-start(bf16[4,120,640]{2,1,0:T(8,128)(2,1)} %broadcast_in_dim.79), calls=%async_computation.7 | async-start | bytes 1228800 | tf_op jit(solution)/shard_map/all_to_all | solution.py:25
  (8 other events, 8.3 us)
Sparse Core Ops, SparseCore 0:
  9.6 41.6 all-gather.7
  52.9 39.5 all-gather.9
  94.2 41.5 all-gather.13
  137.3 38.1 all-gather.11
  177.0 38.2 all-gather.15
  436.7 93.4 reduce-scatter.1
  557.1 135.6 all-reduce.7
where the time goes:
time: 716 us; the launch traced here: 707 us
  waiting for transfers between devices  262 us (37%)
  blocking collectives  121 us (17%)
  local copies, waits for them, and re-layouts  102 us (14%)
  matrix products  101 us (14%)
  starting transfers between devices  62.3 us (9%)
  other arithmetic  41.3 us (6%)
  between operations  17.3 us (2%)
    reduce_scatter x1, waiting for transfers between devices, sent_together(): lax.psum_scatter(both, axis, scatter_dimension=dim, tiled=True)  88.8 us
    psum x1, waiting for transfers between devices, shards(): lax.psum(share_key.astype(jnp.bfloat16), ('ctx', 'tp')).astype(jnp.float32)  65.7 us
    all_to_all x6, waiting for transfers between devices, from_everyone(): return lax.all_to_all(copies, axis, split_axis=0, concat_axis=0, tiled=True)  55.7 us
    all_to_all x2, waiting for transfers between devices, sum_at_owner(): lax.all_to_all(tiles, axis, split_axis=0, concat_axis=0, tiled=True)  43.1 us
    all_to_all x6, starting transfers between devices, from_everyone(): return lax.all_to_all(copies, axis, split_axis=0, concat_axis=0, tiled=True)  39.9 us
    unnamed x2, blocking collectives  33.6 us
    psum x1, blocking collectives, shards(): lax.psum(share_gain_one.astype(jnp.bfloat16), ('ctx', 'tp'))  32.8 us
    all_gather x1, blocking collectives, shards(): lax.all_gather(w_key, 'fsdp', axis=0, tiled=True)  28.6 us
  transfers between devices with their start and end apart: 16, of which 10 were waited for; matrix products, arithmetic and copies ran while one was open for 17% of the time, Pallas kernels for 0%

commit v1 on v0

v1 whole, which is shorter than its diff:
```python
import math

import jax
import jax.numpy as jnp
from jax import lax
from jax.experimental import pallas as pl
from jax.experimental.pallas import tpu as pltpu
from jax.sharding import PartitionSpec as P

QH = 15
KVH = 5
HEAD = 64
GROUP = QH // KVH
EPSILON = 1e-05
ROPE_BASE = 100000.0
SCALE = 1.0 / math.sqrt(HEAD)
NEG = -1e30
BF = jnp.bfloat16
F32 = jnp.float32

HALF_A = 832
HALF_B = 768
HALF_W = 896
FF_HALF = 320
FF_PAD = 384
OUT_HALF = 480
OUT_PAD = 512

CORE_SWAP = [(i, i ^ 1) for i in range(4)]
ROW_SWAP = [(i, i ^ 2) for i in range(4)]
ROW_UP = [(0, 2), (1, 3)]
ROW_DOWN = [(2, 0), (3, 1)]


def dot(a, b, ca, cb):
    return lax.dot_general(a, b, (((ca,), (cb,)), ((), ())), preferred_element_type=F32)


def after(value, *others):
    return lax.optimization_barrier((value, *others))[0]


def from_fsdp(shard):
    copies = jnp.broadcast_to(shard, (lax.axis_size("fsdp"), *shard.shape))
    out = lax.all_to_all(copies, "fsdp", split_axis=0, concat_axis=0, tiled=True)
    return out.reshape(-1, shard.shape[1])


def to_fsdp(full):
    n = lax.axis_size("fsdp")
    tiles = full.reshape(n, full.shape[0] // n, full.shape[1])
    out = lax.all_to_all(tiles, "fsdp", split_axis=0, concat_axis=0, tiled=True)
    return out.astype(F32).sum(axis=0)


def shift(x, by):
    return lax.ppermute(x, "tp", [(i, (i + by) % 4) for i in range(4)])


def tp_blocks(x):
    return [x, shift(x, 1), shift(x, 3), shift(x, 2)]


def tp_sum(own, left, right, far):
    a, b, c = shift(left, 3), shift(right, 1), shift(far, 2)
    return own + a.astype(F32) + b.astype(F32) + c.astype(F32)


def swap_core(x):
    return lax.ppermute(x, "ctx", CORE_SWAP)


def rms_forward(stream, gain_row):
    scale_inv = lax.rsqrt(jnp.mean(stream * stream, -1, keepdims=True) + EPSILON)
    normed = stream * scale_inv
    return scale_inv, normed, (normed * gain_row).astype(BF)


def rms_backward(upstream, scale_inv, normed, gain_row):
    scaled = upstream * gain_row
    inner_mean = jnp.mean(scaled * normed, -1, keepdims=True)
    return scale_inv * (scaled - normed * inner_mean), jnp.sum(upstream * normed, 0)


def turned(x, c, s):
    u1, u2 = x[:32], x[32:]
    return jnp.concatenate([u1 * c - u2 * s, u2 * c + u1 * s], 0)


def turned_back(x, c, s):
    u1, u2 = x[:32], x[32:]
    return jnp.concatenate([u1 * c + u2 * s, u2 * c - u1 * s], 0)


def score_block(keys, queries, b, bias_ref, tri):
    s = dot(keys[b * 256 : (b + 1) * 256], queries, 1, 0) * SCALE
    if b == 0:
        return jnp.where(tri, s, NEG)
    return s + bias_ref[0 if b == 1 else 1]


def triangle():
    u = lax.broadcasted_iota(jnp.int32, (256, 256), 0)
    t = lax.broadcasted_iota(jnp.int32, (256, 256), 1)
    return u <= t


def attend_body(bias, q, k, v, cos, sin, q_out, k_out, att, lse):
    c, s = cos[...], sin[...]
    kb = turned(k[...], c, s).astype(BF)
    k_out[...] = kb
    keys = kb.T
    tri = triangle()
    for g in range(GROUP):
        rows = slice(g * HEAD, (g + 1) * HEAD)
        qb = turned(q[rows, :], c[:, :256], s[:, :256]).astype(BF)
        q_out[rows, :] = qb
        parts = [score_block(keys, qb, b, bias, tri) for b in range(4)]
        tops = [jnp.max(p, 0, keepdims=True) for p in parts]
        top = jnp.maximum(jnp.maximum(tops[0], tops[1]), jnp.maximum(tops[2], tops[3]))
        total = jnp.zeros_like(top)
        out = jnp.zeros((HEAD, 256), F32)
        for b in range(4):
            p = jnp.exp(parts[b] - top)
            total = total + jnp.sum(p, 0, keepdims=True)
            out = out + dot(v[:, b * 256 : (b + 1) * 256], p.astype(BF), 1, 0)
        att[rows, :] = (out / total).astype(BF)
        lse[0, g : g + 1, :] = top + jnp.log(total)
    lse[0, GROUP:, :] = jnp.zeros((8 - GROUP, 256), F32)


def attend_back_body(bias, q, k, v, d, lse, cos, sin, dq, dk, dv):
    c, s = cos[...], sin[...]
    keys, values = k[...].T, v[...].T
    tri = triangle()
    dk_sum = [jnp.zeros((HEAD, 256), F32) for _ in range(4)]
    dv_sum = [jnp.zeros((HEAD, 256), F32) for _ in range(4)]
    for g in range(GROUP):
        rows = slice(g * HEAD, (g + 1) * HEAD)
        qb, db = q[rows, :], d[rows, :]
        log_total = lse[0, g : g + 1, :]
        probs, grads = [], []
        inner = jnp.zeros((1, 256), F32)
        for b in range(4):
            p = jnp.exp(score_block(keys, qb, b, bias, tri) - log_total)
            gp = dot(values[b * 256 : (b + 1) * 256], db, 1, 0)
            inner = inner + jnp.sum(p * gp, 0, keepdims=True)
            probs.append(p)
            grads.append(gp)
        dq_sum = jnp.zeros((HEAD, 256), F32)
        for b in range(4):
            ds = (probs[b] * (grads[b] - inner) * SCALE).astype(BF)
            dv_sum[b] = dv_sum[b] + dot(db, probs[b].astype(BF), 1, 1)
            dk_sum[b] = dk_sum[b] + dot(qb, ds, 1, 1)
            dq_sum = dq_sum + dot(k[:, b * 256 : (b + 1) * 256], ds, 1, 0)
        dq[rows, :] = turned_back(dq_sum, c[:, :256], s[:, :256]).astype(BF)
    for b in range(4):
        cols = slice(b * 256, (b + 1) * 256)
        dk[:, cols] = turned_back(dk_sum[b], c[:, cols], s[:, cols]).astype(BF)
        dv[:, cols] = dv_sum[b].astype(BF)


def per_head(rows, cols):
    return pl.BlockSpec((rows, cols), lambda j: (j, 0))


def whole(rows, cols):
    return pl.BlockSpec((rows, cols), lambda j: (0, 0))


LSE_SPEC = pl.BlockSpec((1, 8, 256), lambda j: (j, 0, 0))
SMEM_SPEC = pl.BlockSpec(memory_space=pltpu.SMEM)


def attend(bias, q, k, v, cos, sin):
    gr = GROUP * HEAD
    return pl.pallas_call(
        attend_body,
        grid=(KVH,),
        in_specs=[SMEM_SPEC, per_head(gr, 256), per_head(HEAD, 1024), per_head(HEAD, 1024), whole(32, 1024), whole(32, 1024)],
        out_specs=[per_head(gr, 256), per_head(HEAD, 1024), per_head(gr, 256), LSE_SPEC],
        out_shape=[
            jax.ShapeDtypeStruct((QH * HEAD, 256), BF),
            jax.ShapeDtypeStruct((KVH * HEAD, 1024), BF),
            jax.ShapeDtypeStruct((QH * HEAD, 256), BF),
            jax.ShapeDtypeStruct((KVH, 8, 256), F32),
        ],
        name="attend",
    )(bias, q, k, v, cos, sin)


def attend_back(bias, q, k, v, d, lse, cos, sin):
    gr = GROUP * HEAD
    return pl.pallas_call(
        attend_back_body,
        grid=(KVH,),
        in_specs=[
            SMEM_SPEC,
            per_head(gr, 256),
            per_head(HEAD, 1024),
            per_head(HEAD, 1024),
            per_head(gr, 256),
            LSE_SPEC,
            whole(32, 1024),
            whole(32, 1024),
        ],
        out_specs=[per_head(gr, 256), per_head(HEAD, 1024), per_head(HEAD, 1024)],
        out_shape=[
            jax.ShapeDtypeStruct((QH * HEAD, 256), BF),
            jax.ShapeDtypeStruct((KVH * HEAD, 1024), BF),
            jax.ShapeDtypeStruct((KVH * HEAD, 1024), BF),
        ],
        name="attend_back",
    )(bias, q, k, v, d, lse, cos, sin)


def shards(
    inputs,
    seq_live,
    positions,
    gain_attn,
    w_query,
    w_key,
    w_value,
    w_out,
    gain_mlp,
    w_gate,
    w_up,
    w_down,
    cotangent,
):
    ctx = lax.axis_index("ctx")
    core = ctx & 1
    first = core == 0
    bias = jnp.where(jnp.stack([core == 1, ctx >= 2]), 0.0, NEG).astype(F32)
    x = inputs[0]
    rows, width = x.shape
    part = w_query.shape[0]

    gains = jnp.pad(jnp.stack([gain_attn, gain_mlp], 1), ((0, 0), (0, HALF_W - HALF_A - 2)))
    half_a = jnp.concatenate([w_query[:, :HALF_A], gains], 1)
    half_b = jnp.concatenate(
        [w_query[:, HALF_A:], w_key, w_value, jnp.zeros((part, HALF_A - HALF_B), BF), gains], 1
    )
    qkv_mine = from_fsdp(jnp.where(first, half_a, half_b))
    qkv_theirs = swap_core(qkv_mine)

    upstream = cotangent[0] * seq_live.astype(F32)[:, None]
    grad_rows = jnp.concatenate(tp_blocks(upstream.astype(BF)), 0)

    earlier = lax.ppermute(x, "ctx", ROW_UP)
    earlier_pos = lax.ppermute(positions, "ctx", ROW_UP)
    beside = swap_core(jnp.stack([x, earlier]))
    beside_pos = swap_core(jnp.concatenate([positions, earlier_pos], 0))
    tokens = jnp.concatenate([x, beside[0], earlier, beside[1]], 0)
    all_pos = jnp.concatenate([positions, beside_pos[:1], earlier_pos, beside_pos[1:]], 1)

    out_part = jnp.where(first, w_out[:, :OUT_HALF], w_out[:, OUT_HALF:])
    out_mine = from_fsdp(after(jnp.pad(out_part, ((0, 0), (0, OUT_PAD - OUT_HALF))), qkv_mine))
    out_theirs = swap_core(out_mine)

    def ff_half(w):
        return jnp.pad(
            jnp.where(first, w[:, :FF_HALF], w[:, FF_HALF:]), ((0, 0), (0, FF_PAD - FF_HALF))
        )

    ff_part = jnp.concatenate([ff_half(w_gate), ff_half(w_up), ff_half(w_down)], 1)
    ff_mine = from_fsdp(after(ff_part, out_mine))
    ff_theirs = swap_core(ff_mine)
    full_gate, full_up, full_down = (
        jnp.concatenate(
            [ff_mine[:, i * FF_PAD : (i + 1) * FF_PAD], ff_theirs[:, i * FF_PAD : (i + 1) * FF_PAD]],
            1,
        )
        for i in range(3)
    )

    inverse = jnp.exp(jnp.arange(32, dtype=F32) * (-2.0 * math.log(ROPE_BASE) / HEAD))
    angles = inverse[:, None] * all_pos.astype(F32)
    cos, sin = jnp.cos(angles), jnp.sin(angles)
    gain_rows = qkv_mine[:, HALF_A : HALF_A + 2].astype(F32).T
    gain_one, gain_two = gain_rows[:1], gain_rows[1:]
    full_a = jnp.where(first, qkv_mine, qkv_theirs)[:, :HALF_A]
    full_b = jnp.where(first, qkv_theirs, qkv_mine)[:, :HALF_B]
    _, _, hidden_all = rms_forward(tokens.astype(F32), gain_one)
    stream = x.astype(F32)
    inv_one, normed_one, hidden_one = rms_forward(stream, gain_one)
    q_lin = jnp.concatenate(
        [dot(full_a, hidden_one, 0, 1), dot(full_b[:, :128], hidden_one, 0, 1)], 0
    )
    k_lin = dot(full_b[:, 128:448], hidden_all, 0, 1)
    values = dot(full_b[:, 448:768], hidden_all, 0, 1).astype(BF)
    queries, keys, attended, lse = attend(bias, q_lin, k_lin, values, cos, sin)

    full_out = jnp.concatenate(
        [
            jnp.where(first, out_mine, out_theirs)[:, :OUT_HALF],
            jnp.where(first, out_theirs, out_mine)[:, :OUT_HALF],
        ],
        1,
    )
    mid = stream + dot(attended, full_out, 0, 0)
    inv_two, normed_two, hidden_two = rms_forward(mid, gain_two)

    mlp_in = jnp.concatenate(tp_blocks(hidden_two), 0)
    gate_pre = dot(mlp_in, full_gate, 1, 0)
    up_pre = dot(mlp_in, full_up, 1, 0)
    sg = jax.nn.sigmoid(gate_pre)
    grad_act = dot(grad_rows, full_down, 1, 0)
    up_back = (grad_act * gate_pre * sg).astype(BF)
    gate_back = (grad_act * up_pre * sg * (1.0 + gate_pre * (1.0 - sg))).astype(BF)
    activated = (gate_pre * sg * up_pre).astype(BF)
    partial_in = dot(gate_back, full_gate, 1, 1) + dot(up_back, full_up, 1, 1)
    partial_in = partial_in.reshape(4, rows, width)
    grad_hidden_two = tp_sum(partial_in[0], *(partial_in[i].astype(BF) for i in (1, 2, 3)))

    partial_out = dot(activated, full_down, 1, 1).reshape(4, rows, width)
    layer_out = mid + tp_sum(partial_out[0], *(partial_out[i].astype(BF) for i in (1, 2, 3)))

    dw_ff = [
        dot(mlp_in, gate_back, 0, 0).astype(BF),
        dot(mlp_in, up_back, 0, 0).astype(BF),
        dot(grad_rows, activated, 0, 0).astype(BF),
    ]
    ff_sent = swap_core(jnp.concatenate([w[:, FF_PAD:] for w in dw_ff], 1))
    ff_kept = jnp.concatenate([w[:, :FF_PAD] for w in dw_ff], 1)
    ff_pair = (ff_kept.astype(F32) + ff_sent.astype(F32)).astype(BF)
    ff_sum = to_fsdp(ff_pair).astype(BF)

    back_two, dgain_two = rms_backward(grad_hidden_two, inv_two, normed_two, gain_two)
    grad_mid = upstream + back_two
    grad_mid_b = grad_mid.astype(BF)
    grad_attended = dot(full_out, grad_mid_b, 1, 1).astype(BF)
    dq, dk, dv = attend_back(bias, queries, keys, values, grad_attended, lse, cos, sin)

    dw_out = dot(attended, grad_mid_b, 1, 0).astype(BF)
    pad_out = ((0, 0), (0, OUT_PAD - OUT_HALF))
    out_l = jnp.pad(dw_out[:, :OUT_HALF], pad_out)
    out_r = jnp.pad(dw_out[:, OUT_HALF:], pad_out)
    out_sent = swap_core(jnp.where(first, out_r, out_l))
    out_pair = (jnp.where(first, out_l, out_r).astype(F32) + out_sent.astype(F32)).astype(BF)
    out_sum = to_fsdp(after(out_pair, ff_sum)).astype(BF)

    dkv = jnp.concatenate([dk, dv], 0)
    from_beside = swap_core(jnp.concatenate([dkv[:, 256:512], dkv[:, 768:1024]], 1))
    own_pair = dkv[:, :256].astype(F32) + from_beside[:, :256].astype(F32)
    earlier_pair = dkv[:, 512:768].astype(F32) + from_beside[:, 256:].astype(F32)
    from_later = lax.ppermute(earlier_pair.astype(BF), "ctx", ROW_DOWN)
    own_kv = (own_pair + from_later.astype(F32)).astype(BF)
    grad_hidden_one = (
        dot(dq[:HALF_A], full_a, 0, 1)
        + dot(dq[HALF_A:], full_b[:, :128], 0, 1)
        + dot(own_kv, full_b[:, 128:], 0, 1)
    )
    back_one, dgain_one = rms_backward(grad_hidden_one, inv_one, normed_one, gain_one)
    grad_input = grad_mid + back_one

    dgains = jnp.pad(
        jnp.stack([dgain_one, dgain_two], 0).T.astype(BF), ((0, 0), (0, HALF_W - HALF_A - 2))
    )
    grad_a = jnp.concatenate([dot(hidden_one, dq[:HALF_A], 0, 1).astype(BF), dgains], 1)
    grad_b = jnp.concatenate(
        [
            dot(hidden_one, dq[HALF_A:], 0, 1).astype(BF),
            dot(hidden_all, dk, 0, 1).astype(BF),
            dot(hidden_all, dv, 0, 1).astype(BF),
            jnp.zeros((width, HALF_A - HALF_B), BF),
            dgains,
        ],
        1,
    )
    qkv_sent = swap_core(jnp.where(first, grad_b, grad_a))
    qkv_pair = (jnp.where(first, grad_a, grad_b).astype(F32) + qkv_sent.astype(F32)).astype(BF)
    qkv_sum = to_fsdp(after(qkv_pair, out_sum)).astype(BF)

    def both_rows(v):
        return v.astype(F32) + lax.ppermute(v, "ctx", ROW_SWAP).astype(F32)

    def all_tp(v):
        for pairs in ([(0, 1), (1, 0), (2, 3), (3, 2)], [(0, 3), (3, 0), (1, 2), (2, 1)]):
            v = (v.astype(F32) + lax.ppermute(v, "tp", pairs).astype(F32)).astype(BF)
        return v

    ff_own = both_rows(ff_sum)
    ff_other = swap_core(ff_own)
    ff_lo, ff_hi = jnp.where(first, ff_own, ff_other), jnp.where(first, ff_other, ff_own)
    dw_gate, dw_up, dw_down = (
        jnp.concatenate([v[:, i * FF_PAD : i * FF_PAD + FF_HALF] for v in (ff_lo, ff_hi)], 1)
        for i in range(3)
    )
    out_own = both_rows(all_tp(out_sum))
    out_other = swap_core(out_own)
    out_lo, out_hi = jnp.where(first, out_own, out_other), jnp.where(first, out_other, out_own)
    dw_out = jnp.concatenate([out_lo[:, :OUT_HALF], out_hi[:, :OUT_HALF]], 1)
    qkv_own = both_rows(all_tp(qkv_sum))
    qkv_other = swap_core(qkv_own)
    got_a, got_b = jnp.where(first, qkv_own, qkv_other), jnp.where(first, qkv_other, qkv_own)
    return (
        layer_out[None],
        grad_input[None],
        got_a[:, HALF_A],
        jnp.concatenate([got_a[:, :HALF_A], got_b[:, :128]], 1),
        got_b[:, 128:448],
        got_b[:, 448:768],
        dw_out,
        got_a[:, HALF_A + 1],
        dw_gate,
        dw_up,
        dw_down,
    )


def solution(mesh):
    seqs, tokens = P(("fsdp", "tp"), "ctx", None), P(("fsdp", "tp"), "ctx")
    row, both = P("fsdp", None), P("fsdp", "tp")
    return jax.shard_map(
        shards,
        mesh=mesh,
        in_specs=(seqs, P(("fsdp", "tp")), tokens, P("fsdp"), row, row, row, row, P("fsdp"), both, both, both, seqs),
        out_specs=(seqs, seqs, P("fsdp"), row, row, row, row, P("fsdp"), both, both, both),
        check_vma=False,
    )
```

time: 716 us -> 390 us (0.54)
  waiting for transfers between devices: 262 us -> 132 us
  blocking collectives: 121 us -> 0 us
  local copies, waits for them, and re-layouts: 102 us -> 42.6 us
  matrix products: 101 us -> 43.7 us
  Pallas kernels: 0 us -> 27.9 us
  starting transfers between devices: 62.3 us -> 84.2 us
  between operations: 17.3 us -> 2.45 us
  other arithmetic: 41.3 us -> 49.6 us
    reduce_scatter x1 -> x0, waiting for transfers between devices: 88.8 us -> none  [sent_together(): lax.psum_scatter(both, axis, scatter_dimension=dim, tiled=True)]
    ppermute x0 -> x34, waiting for transfers between devices: none -> 76 us  [the longest x12 41.1 us: shift(): return lax.ppermute(x, 'tp', [(i, (i + by) % 4) for i in range(4)])]
    psum x1 -> x0, waiting for transfers between devices: 65.7 us -> none  [shards(): lax.psum(share_key.astype(jnp.bfloat16), ('ctx', 'tp')).astype(jnp.float32)]
    dot_general x51 -> x23, matrix products: 101 us -> 43.7 us  [dot(): lax.dot_general(a, b, (((ca,), (cb,)), ((), ())), preferred_element_type=...]
    ppermute x0 -> x34, starting transfers between devices: none -> 56.1 us  [the longest x12 26.4 us: shift(): return lax.ppermute(x, 'tp', [(i, (i + by) % 4) for i in range(4)])]
    all_gather x2 -> x0, blocking collectives: 54.6 us -> none  [the longest x1 28.6 us: shards(): lax.all_gather(w_key, 'fsdp', axis=0, tiled=True)]
    all_to_all x9 -> x6, waiting for transfers between devices: 100 us -> 55.6 us  [the longest x3 35.1 us: to_fsdp(): out = lax.all_to_all(tiles, 'fsdp', split_axis=0, concat_axis=0, tiled=True)]
    all_to_all x9 -> x6, starting transfers between devices: 61.7 us -> 28.1 us  [the longest x3 15.8 us: from_fsdp(): lax.all_to_all(copies, 'fsdp', split_axis=0, concat_axis=0, tiled=True)]
  transfers between devices with their start and end apart: 16 -> 40, of which waited for: 10 -> 20; matrix products, arithmetic and copies ran while one was open for 17% -> 26% of each run, Pallas kernels for 0% -> 7%
where the time goes in v1:
time: 390 us; the launch traced here: 382 us
  waiting for transfers between devices  132 us (34%)
  starting transfers between devices  84.2 us (22%)
  other arithmetic  49.6 us (13%)
  matrix products  43.7 us (11%)
  local copies, waits for them, and re-layouts  42.6 us (11%)
  Pallas kernels  27.9 us (7%)
    dot_general x23, matrix products, dot(): lax.dot_general(a, b, (((ca,), (cb,)), ((), ())), preferred_element_type=...  43.7 us
    ppermute x12, waiting for transfers between devices, shift(): return lax.ppermute(x, 'tp', [(i, (i + by) % 4) for i in range(4)])  41.1 us
    all_to_all x3, waiting for transfers between devices, to_fsdp(): out = lax.all_to_all(tiles, 'fsdp', split_axis=0, concat_axis=0, tiled=True)  35.1 us
    ppermute x12, starting transfers between devices, shift(): return lax.ppermute(x, 'tp', [(i, (i + by) % 4) for i in range(4)])  26.4 us
    all_to_all x3, waiting for transfers between devices, from_fsdp(): lax.all_to_all(copies, 'fsdp', split_axis=0, concat_axis=0, tiled=True)  20.5 us
    pallas_call x1, Pallas kernels, attend_back(): pl.pallas_call(attend_back_body, grid=(KVH,), in_specs=[SMEM_SPEC, per_he...  16.8 us
    ppermute x1, waiting for transfers between devices, shards(): earlier = lax.ppermute(x, 'ctx', ROW_UP)  16.4 us
    all_to_all x3, starting transfers between devices, from_fsdp(): lax.all_to_all(copies, 'fsdp', split_axis=0, concat_axis=0, tiled=True)  15.8 us
  transfers between devices with their start and end apart: 40, of which 20 were waited for; matrix products, arithmetic and copies ran while one was open for 26% of the time, Pallas kernels for 7%

profile of v1, /device:TPU:1, one launch (start us, length us, event | category | flops | bytes accessed | tf_op | source)
XLA Modules:
  0.0 382.2 jit_solution(12675688288750068069)
XLA Ops:
  7.0 7.0 %all-to-all-start = ((bf16[8,120,896]{2,1,0:T(8,128)(2,1)}), bf16[8,120,896]{2,1,0:T(8,128)(2,1)}, u32[]{:S(2)}, u32[]{:S(2)}) async-start(bf16[8,120,896]{2,1,0:T(8,128)(2,1)} %broadcast_in_dim.39), calls=%async_computation | async-start | bytes 3440640 | tf_op jit(solution)/shard_map/all_to_all | solution.py:45
  15.6 2.7 collective-permute-start.15
  19.8 4.5 %collective-permute-start.3 = (s32[1,256]{1,0:T(1,128)S(1)}, s32[1,256]{1,0:T(1,128)S(1)}, u32[]{:S(2)}, u32[]{:S(2)}) collective-permute-start(s32[1,256]{1,0:T(1,128)S(1)} %copy-done.36), channel_id=1, source_target_pairs={{0,8},{4,12},{1,9},{5,13},{2,10},{6,14},{3,11},{7,15},{16,24},{20,... | collective-permute-start | bytes 3080 | tf_op jit(solution)/shard_map/ppermute | solution.py:252
  26.3 16.4 %collective-permute-done.1 = bf16[256,960]{0,1:T(8,128)(2,1)S(1)} collective-permute-done((bf16[256,960]{0,1:T(8,128)(2,1)S(1)}, bf16[256,960]{0,1:T(8,128)(2,1)S(1)}, u32[]{:S(2)}, u32[]{:S(2)}) %collective-permute-start.1) | collective-permute-done | bytes 491552 | tf_op jit(solution)/shard_map/ppermute | solution.py:251
  46.8 5.2 %all-to-all-start.1 = ((bf16[8,120,512]{2,1,0:T(8,128)(2,1)}), bf16[8,120,512]{2,1,0:T(8,128)(2,1)}, u32[]{:S(2)}, u32[]{:S(2)}) async-start(bf16[8,120,512]{2,1,0:T(8,128)(2,1)} %broadcast_in_dim.40), calls=%async_computation.1 | async-start | bytes 1966080 | tf_op jit(solution)/shard_map/all_to_all | solution.py:45
  54.8 11.5 %all-to-all-done.1 = bf16[8,120,512]{2,1,0:T(8,128)(2,1)} async-done(((bf16[8,120,512]{2,1,0:T(8,128)(2,1)}), bf16[8,120,512]{2,1,0:T(8,128)(2,1)}, u32[]{:S(2)}, u32[]{:S(2)}) %all-to-all-start.1) | async-done | bytes 983072 | tf_op jit(solution)/shard_map/all_to_all | solution.py:45
  67.9 3.7 all-to-all-start.2
  74.1 3.7 copy.90
  79.9 1.8 fusion.2
  82.5 3.7 copy.91
  86.1 3.1 broadcast_select_fusion
  90.0 9.0 %all-to-all-done.2 = bf16[8,120,1152]{2,1,0:T(8,128)(2,1)S(1)} async-done(((bf16[8,120,1152]{2,1,0:T(8,128)(2,1)}), bf16[8,120,1152]{2,1,0:T(8,128)(2,1)S(1)}, u32[]{:S(2)}, u32[]{:S(2)}) %all-to-all-start.2) | async-done | bytes 2211872 | tf_op jit(solution)/shard_map/all_to_all | solution.py:45
  102.6 3.4 convolution_convert_fusion.7.v
  106.0 1.9 fusion.32.k
  107.9 11.1 %attend.1 = (bf16[960,256]{1,0:T(8,128)(2,1)}, bf16[320,1024]{1,0:T(8,128)(2,1)}, bf16[960,256]{1,0:T(8,128)(2,1)}, f32[5,8,256]{2,1,0:T(8,128)}) custom-call(f32[2]{0:T(128)} %add_select_fusion.bias, f32[960,256]{1,0:T(8,128)} %pad_maximum_fusion.11.q, f32[320,1024]{1,0:T(8,128)} %fusion.32.k, bf16[320,1024]{1,0:T(8,128)(2,1)} %convolution_convert_fusion.7.v, ...), custom_call_target="tpu_custom_call" | custom-call | tf_op jit(solution)/shard_map/attend/pallas_call | solution.py:177
  122.6 2.8 collective-permute-start.8
  127.4 1.8 fusion.68
  129.2 3.4 fusion.26
  132.6 4.4 %collective-permute-done.8 = bf16[256,960]{0,1:T(8,128)(2,1)S(1)} collective-permute-done((bf16[256,960]{0,1:T(8,128)(2,1)S(1)}, bf16[256,960]{0,1:T(8,128)(2,1)S(1)}, u32[]{:S(2)}, u32[]{:S(2)}) %collective-permute-start.8) | collective-permute-done | bytes 491552 | tf_op jit(solution)/shard_map/ppermute | solution.py:57
  137.0 10.6 %collective-permute-done.7 = bf16[256,960]{0,1:T(8,128)(2,1)S(1)} collective-permute-done((bf16[256,960]{0,1:T(8,128)(2,1)S(1)}, bf16[256,960]{0,1:T(8,128)(2,1)S(1)}, u32[]{:S(2)}, u32[]{:S(2)}) %collective-permute-start.7) | collective-permute-done | bytes 491552 | tf_op jit(solution)/shard_map/ppermute | solution.py:57
  147.9 1.9 fusion.29
  149.8 3.3 multiply_convert_fusion.1
  153.0 3.2 convolution_convert_fusion.2
  157.2 1.7 fusion.28
  158.9 1.7 convolution_convert_fusion.3
  161.7 1.9 convolution_convert_fusion.4
  164.7 1.7 fusion.80
  166.5 2.6 collective-permute-start.16
  173.0 1.7 fusion.81
  174.9 2.2 collective-permute-start.10
  177.1 3.0 collective-permute-done.16
  182.6 10.3 %collective-permute-start.11 = (bf16[256,960]{0,1:T(8,128)(2,1)S(1)}, bf16[256,960]{0,1:T(8,128)(2,1)S(1)}, u32[]{:S(2)}, u32[]{:S(2)}) collective-permute-start(bf16[256,960]{0,1:T(8,128)(2,1)S(1)} %get-tuple-element.133), channel_id=1, source_target_pairs={{0,1},{1,2},{2,3},{3,0},{4,5},{5,6},{6,7},{7,4},{8,9},{9,10},{10,1... | collective-permute-start | bytes 1474568 | tf_op jit(solution)/shard_map/ppermute | solution.py:57
  192.9 2.4 collective-permute-done.17
  195.9 5.3 %collective-permute-done.10 = bf16[256,960]{0,1:T(8,128)(2,1)S(1)} collective-permute-done((bf16[256,960]{0,1:T(8,128)(2,1)S(1)}, bf16[256,960]{0,1:T(8,128)(2,1)S(1)}, u32[]{:S(2)}, u32[]{:S(2)}) %collective-permute-start.10) | collective-permute-done | bytes 491552 | tf_op jit(solution)/shard_map/ppermute | solution.py:57
  201.2 1.7 collective-permute-done.12
  202.8 12.4 %collective-permute-done.11 = bf16[256,960]{0,1:T(8,128)(2,1)S(1)} collective-permute-done((bf16[256,960]{0,1:T(8,128)(2,1)S(1)}, bf16[256,960]{0,1:T(8,128)(2,1)S(1)}, u32[]{:S(2)}, u32[]{:S(2)}) %collective-permute-start.11) | collective-permute-done | bytes 491552 | tf_op jit(solution)/shard_map/ppermute | solution.py:57
  218.2 16.8 %attend_back.1 = (bf16[960,256]{1,0:T(8,128)(2,1)}, bf16[320,1024]{1,0:T(8,128)(2,1)}, bf16[320,1024]{1,0:T(8,128)(2,1)}) custom-call(f32[2]{0:T(128)} %add_select_fusion.bias, bf16[960,256]{1,0:T(8,128)(2,1)} %get-tuple-element.25.q, bf16[320,1024]{1,0:T(8,128)(2,1)} %get-tuple-element.26.k, bf16[320,1024]{1,0:T(8,128)(2,1)} %convolution_convert_fusion.7.v, ...), custom_call_target="tpu_custom_call" | custom-call | tf_op jit(solution)/shard_map/attend_back/pallas_call | solution.py:194
  235.0 2.0 convolution_convert_fusion.9
  248.0 9.5 %collective-permute-done.20 = bf16[640,256]{1,0:T(8,128)(2,1)S(1)} collective-permute-done((bf16[640,256]{1,0:T(8,128)(2,1)S(1)}, bf16[640,256]{1,0:T(8,128)(2,1)S(1)}, u32[]{:S(2)}, u32[]{:S(2)}) %collective-permute-start.20) | collective-permute-done | bytes 327712 | tf_op jit(solution)/shard_map/ppermute | solution.py:348
  259.1 3.7 add_convert_fusion
  262.8 4.4 %all-to-all-start.3 = ((bf16[8,120,1152]{2,1,0:T(8,128)(2,1)}), bf16[8,120,1152]{2,1,0:T(8,128)(2,1)}, u32[]{:S(2)}, u32[]{:S(2)}) async-start(bf16[8,120,1152]{2,1,0:T(8,128)(2,1)} %bitcast.60), calls=%async_computation.3 | async-start | bytes 4423680 | tf_op jit(solution)/shard_map/all_to_all | solution.py:52
  267.2 4.8 %fusion.18 = (bf16[960]{0:T(1024)(128)(2,1)S(1)}, f32[256]{0:T(256)S(1)}, f32[256,960]{0,1:T(8,128)}) fusion(f32[256]{0:T(256)S(1)} %copy-done.35, bf16[1,256,960]{1,2,0:T(8,128)(2,1)S(1)} %copy-done, f32[960]{0:T(1024)S(1)} %copy-done.32, f32[256,960]{0,1:T(8,128)} %fusion.10, f32[256,960]{0,1:T(8,128)} %fusion.47, bf16[960,896]{0,1:T(8,128)(2,1)} %copy.91, ...), kind=kOutput, calls=%fused_computation.54 | convolution fusion | flops 411953984 | bytes 7282305 | tf_op jit(solution)/shard_map/dot_general | solution.py:36
  273.3 2.1 broadcast_select_fusion.1
  275.4 3.8 copy.95
  280.3 2.8 broadcast_select_fusion.4
  283.1 11.5 %all-to-all-done.3 = bf16[8,120,1152]{2,1,0:T(8,128)(2,1)} async-done(((bf16[8,120,1152]{2,1,0:T(8,128)(2,1)}), bf16[8,120,1152]{2,1,0:T(8,128)(2,1)}, u32[]{:S(2)}, u32[]{:S(2)}) %all-to-all-start.3) | async-done | bytes 2211872 | tf_op jit(solution)/shard_map/all_to_all | solution.py:52
  294.6 2.0 reduce_sum.106
  296.7 3.2 add_convert_fusion.2
  299.9 3.7 copy.96
  303.6 4.2 %all-to-all-start.4 = ((bf16[8,120,512]{2,1,0:T(8,128)(2,1)}), bf16[8,120,512]{2,1,0:T(8,128)(2,1)}, u32[]{:S(2)}, u32[]{:S(2)}) async-start(bf16[8,120,512]{2,1,0:T(8,128)(2,1)} %bitcast.65), calls=%async_computation.4 | async-start | bytes 1966080 | tf_op jit(solution)/shard_map/all_to_all | solution.py:52
  307.9 1.8 convert_add_fusion.1
  310.6 4.6 %add_convert_fusion.1 = bf16[960,896]{0,1:T(8,128)(2,1)} fusion(bf16[960,896]{0,1:T(8,128)(2,1)} %copy.96, bf16[960,896]{0,1:T(8,128)(2,1)} %copy-done.4, pred[]{:T(512)S(6)} %eq.7, bf16[960,64]{0,1:T(8,128)(2,1)} %copy-done.20, bf16[960,832]{0,1:T(8,128)(2,1)S(1)} %convolution_convert_fusion.1), kind=kLoop, calls=%fused_computation.6 | loop fusion | flops 7741440 | bytes 6881281 | tf_op jit(solution)/shard_map/convert_element_type | solution.py:373
  315.2 6.9 %all-to-all-done.4 = bf16[8,120,512]{2,1,0:T(8,128)(2,1)} async-done(((bf16[8,120,512]{2,1,0:T(8,128)(2,1)}), bf16[8,120,512]{2,1,0:T(8,128)(2,1)}, u32[]{:S(2)}, u32[]{:S(2)}) %all-to-all-start.4) | async-done | bytes 983072 | tf_op jit(solution)/shard_map/all_to_all | solution.py:52
  322.1 2.0 reduce_sum.107
  324.1 3.8 copy.97
  327.9 3.6 all-to-all-start.5
  331.5 2.4 fusion.17
  337.1 16.6 %all-to-all-done.5 = bf16[8,120,896]{2,1,0:T(8,128)(2,1)S(1)} async-done(((bf16[8,120,896]{2,1,0:T(8,128)(2,1)}), bf16[8,120,896]{2,1,0:T(8,128)(2,1)S(1)}, u32[]{:S(2)}, u32[]{:S(2)}) %all-to-all-start.5) | async-done | bytes 1720352 | tf_op jit(solution)/shard_map/all_to_all | solution.py:52
  354.9 5.1 %collective-permute-done.24 = bf16[120,896]{1,0:T(8,128)(2,1)S(1)} collective-permute-done((bf16[120,896]{1,0:T(8,128)(2,1)S(1)}, bf16[120,896]{1,0:T(8,128)(2,1)S(1)}, u32[]{:S(2)}, u32[]{:S(2)}) %collective-permute-start.24) | collective-permute-done | bytes 215072 | tf_op jit(solution)/shard_map/ppermute | solution.py:381
  360.3 3.1 collective-permute-start.30
  363.4 3.2 collective-permute-done.25
  366.7 3.1 collective-permute-start.26
  369.9 2.9 collective-permute-start.31
  373.2 3.6 collective-permute-start.27
  (217 shorter events, 73.8 us)
Async XLA Ops:
  7.0 7.7 %copy-start.11 = (f32[1,256,960]{1,2,0:T(8,128)S(1)}, f32[1,256,960]{1,2,0:T(8,128)}, u32[]{:S(2)}) copy-start(f32[1,256,960]{1,2,0:T(8,128)} %param.25) | copy-start | bytes 2949124
  7.0 12.9 %copy-start.36 = (s32[1,256]{1,0:T(1,128)S(1)}, s32[1,256]{1,0:T(1,128)}, u32[]{:S(2)}) copy-start(s32[1,256]{1,0:T(1,128)} %param.15) | copy-start | bytes 3076
  7.0 17.4 %copy-start = (bf16[1,256,960]{1,2,0:T(8,128)(2,1)S(1)}, bf16[1,256,960]{1,2,0:T(8,128)(2,1)}, u32[]{:S(2)}) copy-start(bf16[1,256,960]{1,2,0:T(8,128)(2,1)} %param.13) | copy-start | bytes 1474564
  7.0 18.7 %copy-start.29 = (bf16[120,640]{1,0:T(8,128)(2,1)S(1)}, bf16[120,640]{1,0:T(8,128)(2,1)}, u32[]{:S(2)}) copy-start(bf16[120,640]{1,0:T(8,128)(2,1)} %param.22) | copy-start | bytes 460804
  7.0 18.8 %copy-start.26 = (bf16[120,960]{1,0:T(8,128)(2,1)S(1)}, bf16[120,960]{1,0:T(8,128)(2,1)}, u32[]{:S(2)}) copy-start(bf16[120,960]{1,0:T(8,128)(2,1)} %param.20) | copy-start | bytes 691204
  7.0 38.8 %all-to-all-start = ((bf16[8,120,896]{2,1,0:T(8,128)(2,1)}), bf16[8,120,896]{2,1,0:T(8,128)(2,1)}, u32[]{:S(2)}, u32[]{:S(2)}) async-start(bf16[8,120,896]{2,1,0:T(8,128)(2,1)} %broadcast_in_dim.39), calls=%async_computation | async-start | bytes 3440640 | tf_op jit(solution)/shard_map/all_to_all | solution.py:45
  14.0 12.1 %copy-start.27 = (bf16[120,640]{1,0:T(8,128)(2,1)S(1)}, bf16[120,640]{1,0:T(8,128)(2,1)}, u32[]{:S(2)}) copy-start(bf16[120,640]{1,0:T(8,128)(2,1)} %param.24) | copy-start | bytes 460804
  14.0 12.1 %copy-start.28 = (bf16[120,640]{1,0:T(8,128)(2,1)S(1)}, bf16[120,640]{1,0:T(8,128)(2,1)}, u32[]{:S(2)}) copy-start(bf16[120,640]{1,0:T(8,128)(2,1)} %param.23) | copy-start | bytes 460804
  15.6 110.0 %collective-permute-start.15 = (bf16[256,960]{0,1:T(8,128)(2,1)}, bf16[256,960]{0,1:T(8,128)(2,1)}, u32[]{:S(2)}, u32[]{:S(2)}) collective-permute-start(bf16[256,960]{0,1:T(8,128)(2,1)} %bitcast_convert_fusion), channel_id=1, source_target_pairs={{0,2},{1,3},{2,0},{3,1},{4,6},{5,7},{6,4},{7,5},{8,10},{9,11},{10,... | collective-permute-start | bytes 1474568 | tf_op jit(solution)/shard_map/ppermute | solution.py:57
  18.4 110.8 %collective-permute-start.14 = (bf16[256,960]{0,1:T(8,128)(2,1)}, bf16[256,960]{0,1:T(8,128)(2,1)}, u32[]{:S(2)}, u32[]{:S(2)}) collective-permute-start(bf16[256,960]{0,1:T(8,128)(2,1)} %bitcast_convert_fusion), channel_id=1, source_target_pairs={{0,3},{1,0},{2,1},{3,2},{4,7},{5,4},{6,5},{7,6},{8,11},{9,8},{10,9... | collective-permute-start | bytes 1474568 | tf_op jit(solution)/shard_map/ppermute | solution.py:57
  19.2 109.9 %collective-permute-start.13 = (bf16[256,960]{0,1:T(8,128)(2,1)}, bf16[256,960]{0,1:T(8,128)(2,1)}, u32[]{:S(2)}, u32[]{:S(2)}) collective-permute-start(bf16[256,960]{0,1:T(8,128)(2,1)} %bitcast_convert_fusion), channel_id=1, source_target_pairs={{0,1},{1,2},{2,3},{3,0},{4,5},{5,6},{6,7},{7,4},{8,9},{9,10},{10,1... | collective-permute-start | bytes 1474568 | tf_op jit(solution)/shard_map/ppermute | solution.py:57
  19.8 32.2 %collective-permute-start.3 = (s32[1,256]{1,0:T(1,128)S(1)}, s32[1,256]{1,0:T(1,128)S(1)}, u32[]{:S(2)}, u32[]{:S(2)}) collective-permute-start(s32[1,256]{1,0:T(1,128)S(1)} %copy-done.36), channel_id=1, source_target_pairs={{0,8},{4,12},{1,9},{5,13},{2,10},{6,14},{3,11},{7,15},{16,24},{20,... | collective-permute-start | bytes 3080 | tf_op jit(solution)/shard_map/ppermute | solution.py:252
  24.4 18.3 %collective-permute-start.1 = (bf16[256,960]{0,1:T(8,128)(2,1)S(1)}, bf16[256,960]{0,1:T(8,128)(2,1)S(1)}, u32[]{:S(2)}, u32[]{:S(2)}) collective-permute-start(bf16[256,960]{0,1:T(8,128)(2,1)S(1)} %bitcast.57), channel_id=1, source_target_pairs={{0,8},{4,12},{1,9},{5,13},{2,10},{6,14},{3,11},{7,15},{16,24},{20,... | collective-permute-start | bytes 1474568 | tf_op jit(solution)/shard_map/ppermute | solution.py:251
  43.7 27.9 %collective-permute-start.2 = (bf16[2,256,960]{1,2,0:T(8,128)(2,1)}, bf16[2,256,960]{1,2,0:T(8,128)(2,1)}, u32[]{:S(2)}, u32[]{:S(2)}) collective-permute-start(bf16[2,256,960]{1,2,0:T(8,128)(2,1)} %pad_maximum_fusion.12), channel_id=1, source_target_pairs={{0,4},{4,0},{8,12},{12,8},{1,5},{5,1},{9,13},{13,9},{2,6},{6,2},{1... | collective-permute-start | bytes 2949128 | tf_op jit(solution)/shard_map/ppermute | solution.py:70
  46.8 19.5 %all-to-all-start.1 = ((bf16[8,120,512]{2,1,0:T(8,128)(2,1)}), bf16[8,120,512]{2,1,0:T(8,128)(2,1)}, u32[]{:S(2)}, u32[]{:S(2)}) async-start(bf16[8,120,512]{2,1,0:T(8,128)(2,1)} %broadcast_in_dim.40), calls=%async_computation.1 | async-start | bytes 1966080 | tf_op jit(solution)/shard_map/all_to_all | solution.py:45
  52.0 1.2 collective-permute-start.4
  53.3 29.2 %collective-permute-start = (bf16[960,896]{1,0:T(8,128)(2,1)}, bf16[960,896]{1,0:T(8,128)(2,1)}, u32[]{:S(2)}, u32[]{:S(2)}) collective-permute-start(bf16[960,896]{1,0:T(8,128)(2,1)} %bitcast.5), channel_id=1, source_target_pairs={{0,4},{4,0},{8,12},{12,8},{1,5},{5,1},{9,13},{13,9},{2,6},{6,2},{1... | collective-permute-start | bytes 5160968 | tf_op jit(solution)/shard_map/ppermute | solution.py:70
  67.9 31.1 %all-to-all-start.2 = ((bf16[8,120,1152]{2,1,0:T(8,128)(2,1)}), bf16[8,120,1152]{2,1,0:T(8,128)(2,1)S(1)}, u32[]{:S(2)}, u32[]{:S(2)}) async-start(bf16[8,120,1152]{2,1,0:T(8,128)(2,1)} %broadcast_in_dim.41), calls=%async_computation.2 | async-start | bytes 4423680 | tf_op jit(solution)/shard_map/all_to_all | solution.py:45
  81.7 37.4 %collective-permute-start.5 = (bf16[960,512]{1,0:T(8,128)(2,1)}, bf16[960,512]{1,0:T(8,128)(2,1)}, u32[]{:S(2)}, u32[]{:S(2)}) collective-permute-start(bf16[960,512]{1,0:T(8,128)(2,1)} %bitcast.14), channel_id=1, source_target_pairs={{0,4},{4,0},{8,12},{12,8},{1,5},{5,1},{9,13},{13,9},{2,6},{6,2},{1... | collective-permute-start | bytes 2949128 | tf_op jit(solution)/shard_map/ppermute | solution.py:70
  86.1 3.1 copy-start.5
  86.1 3.1 copy-start.6
  86.1 3.1 copy-start.31
  86.1 3.1 copy-start.34
  99.0 3.6 copy-start.16
  99.0 27.6 %collective-permute-start.9 = (bf16[960,1152]{1,0:T(8,128)(2,1)S(1)}, bf16[960,1152]{1,0:T(8,128)(2,1)}, u32[]{:S(2)}, u32[]{:S(2)}) collective-permute-start(bf16[960,1152]{1,0:T(8,128)(2,1)S(1)} %bitcast.61), channel_id=1, source_target_pairs={{0,4},{4,0},{8,12},{12,8},{1,5},{5,1},{9,13},{13,9},{2,6},{6,2},{1... | collective-permute-start | bytes 6635528 | tf_op jit(solution)/shard_map/ppermute | solution.py:70
  102.6 3.4 copy-start.18
  122.6 14.4 %collective-permute-start.8 = (bf16[256,960]{0,1:T(8,128)(2,1)S(1)}, bf16[256,960]{0,1:T(8,128)(2,1)S(1)}, u32[]{:S(2)}, u32[]{:S(2)}) collective-permute-start(bf16[256,960]{0,1:T(8,128)(2,1)S(1)} %multiply_convert_fusion.3), channel_id=1, source_target_pairs={{0,2},{1,3},{2,0},{3,1},{4,6},{5,7},{6,4},{7,5},{8,10},{9,11},{10,... | collective-permute-start | bytes 1474568 | tf_op jit(solution)/shard_map/ppermute | solution.py:57
  125.7 21.9 %collective-permute-start.7 = (bf16[256,960]{0,1:T(8,128)(2,1)S(1)}, bf16[256,960]{0,1:T(8,128)(2,1)S(1)}, u32[]{:S(2)}, u32[]{:S(2)}) collective-permute-start(bf16[256,960]{0,1:T(8,128)(2,1)S(1)} %multiply_convert_fusion.3), channel_id=1, source_target_pairs={{0,3},{1,0},{2,1},{3,2},{4,7},{5,4},{6,5},{7,6},{8,11},{9,8},{10,9... | collective-permute-start | bytes 1474568 | tf_op jit(solution)/shard_map/ppermute | solution.py:57
  126.6 21.3 %collective-permute-start.6 = (bf16[256,960]{0,1:T(8,128)(2,1)S(1)}, bf16[256,960]{0,1:T(8,128)(2,1)S(1)}, u32[]{:S(2)}, u32[]{:S(2)}) collective-permute-start(bf16[256,960]{0,1:T(8,128)(2,1)S(1)} %multiply_convert_fusion.3), channel_id=1, source_target_pairs={{0,1},{1,2},{2,3},{3,0},{4,5},{5,6},{6,7},{7,4},{8,9},{9,10},{10,1... | collective-permute-start | bytes 1474568 | tf_op jit(solution)/shard_map/ppermute | solution.py:57
  166.5 13.6 %collective-permute-start.16 = (bf16[256,960]{0,1:T(8,128)(2,1)S(1)}, bf16[256,960]{0,1:T(8,128)(2,1)S(1)}, u32[]{:S(2)}, u32[]{:S(2)}) collective-permute-start(bf16[256,960]{0,1:T(8,128)(2,1)S(1)} %get-tuple-element.128), channel_id=1, source_target_pairs={{0,3},{1,0},{2,1},{3,2},{4,7},{5,4},{6,5},{7,6},{8,11},{9,8},{10,9... | collective-permute-start | bytes 1474568 | tf_op jit(solution)/shard_map/ppermute | solution.py:57
  169.1 13.6 %collective-permute-start.18 = (bf16[256,960]{0,1:T(8,128)(2,1)S(1)}, bf16[256,960]{0,1:T(8,128)(2,1)S(1)}, u32[]{:S(2)}, u32[]{:S(2)}) collective-permute-start(bf16[256,960]{0,1:T(8,128)(2,1)S(1)} %get-tuple-element.129), channel_id=1, source_target_pairs={{0,2},{1,3},{2,0},{3,1},{4,6},{5,7},{6,4},{7,5},{8,10},{9,11},{10,... | collective-permute-start | bytes 1474568 | tf_op jit(solution)/shard_map/ppermute | solution.py:57
  169.6 25.7 %collective-permute-start.17 = (bf16[256,960]{0,1:T(8,128)(2,1)S(1)}, bf16[256,960]{0,1:T(8,128)(2,1)S(1)}, u32[]{:S(2)}, u32[]{:S(2)}) collective-permute-start(bf16[256,960]{0,1:T(8,128)(2,1)S(1)} %get-tuple-element.130), channel_id=1, source_target_pairs={{0,1},{1,2},{2,3},{3,0},{4,5},{5,6},{6,7},{7,4},{8,9},{9,10},{10,1... | collective-permute-start | bytes 1474568 | tf_op jit(solution)/shard_map/ppermute | solution.py:57
  171.7 87.4 %collective-permute-start.23 = (bf16[960,1152]{1,0:T(8,128)(2,1)}, bf16[960,1152]{1,0:T(8,128)(2,1)}, u32[]{:S(2)}, u32[]{:S(2)}) collective-permute-start(bf16[960,1152]{1,0:T(8,128)(2,1)} %pad_maximum_fusion), channel_id=1, source_target_pairs={{0,4},{4,0},{8,12},{12,8},{1,5},{5,1},{9,13},{13,9},{2,6},{6,2},{1... | collective-permute-start | bytes 6635528 | tf_op jit(solution)/shard_map/ppermute | solution.py:70
  174.9 26.3 %collective-permute-start.10 = (bf16[256,960]{0,1:T(8,128)(2,1)S(1)}, bf16[256,960]{0,1:T(8,128)(2,1)S(1)}, u32[]{:S(2)}, u32[]{:S(2)}) collective-permute-start(bf16[256,960]{0,1:T(8,128)(2,1)S(1)} %get-tuple-element.131), channel_id=1, source_target_pairs={{0,3},{1,0},{2,1},{3,2},{4,7},{5,4},{6,5},{7,6},{8,11},{9,8},{10,9... | collective-permute-start | bytes 1474568 | tf_op jit(solution)/shard_map/ppermute | solution.py:57
  180.1 22.7 %collective-permute-start.12 = (bf16[256,960]{0,1:T(8,128)(2,1)S(1)}, bf16[256,960]{0,1:T(8,128)(2,1)S(1)}, u32[]{:S(2)}, u32[]{:S(2)}) collective-permute-start(bf16[256,960]{0,1:T(8,128)(2,1)S(1)} %get-tuple-element.132), channel_id=1, source_target_pairs={{0,2},{1,3},{2,0},{3,1},{4,6},{5,7},{6,4},{7,5},{8,10},{9,11},{10,... | collective-permute-start | bytes 1474568 | tf_op jit(solution)/shard_map/ppermute | solution.py:57
  182.6 32.6 %collective-permute-start.11 = (bf16[256,960]{0,1:T(8,128)(2,1)S(1)}, bf16[256,960]{0,1:T(8,128)(2,1)S(1)}, u32[]{:S(2)}, u32[]{:S(2)}) collective-permute-start(bf16[256,960]{0,1:T(8,128)(2,1)S(1)} %get-tuple-element.133), channel_id=1, source_target_pairs={{0,1},{1,2},{2,3},{3,0},{4,5},{5,6},{6,7},{7,4},{8,9},{9,10},{10,1... | collective-permute-start | bytes 1474568 | tf_op jit(solution)/shard_map/ppermute | solution.py:57
  195.3 20.0 %copy-start.12 = (f32[1,256,960]{1,2,0:T(8,128)S(1)}, f32[1,256,960]{1,2,0:T(8,128)}, u32[]{:S(2)}) copy-start(f32[1,256,960]{1,2,0:T(8,128)} %param.25) | copy-start | bytes 2949124
  218.2 16.8 %copy-start.32 = (f32[960]{0:T(1024)S(1)}, f32[960]{0:T(1024)}, u32[]{:S(2)}) copy-start(f32[960]{0:T(1024)} %copy-done.30) | copy-start | bytes 11524
  218.2 16.8 %copy-start.35 = (f32[256]{0:T(256)S(1)}, f32[256]{0:T(256)}, u32[]{:S(2)}) copy-start(f32[256]{0:T(256)} %add_rsqrt_fusion.2) | copy-start | bytes 3076
  235.0 3.2 copy-start.21
  238.3 5.9 %collective-permute-start.19 = (bf16[640,512]{1,0:T(8,128)(2,1)S(1)}, bf16[640,512]{1,0:T(8,128)(2,1)S(1)}, u32[]{:S(2)}, u32[]{:S(2)}) collective-permute-start(bf16[640,512]{1,0:T(8,128)(2,1)S(1)} %pad_maximum_fusion.19), channel_id=1, source_target_pairs={{0,4},{4,0},{8,12},{12,8},{1,5},{5,1},{9,13},{13,9},{2,6},{6,2},{1... | collective-permute-start | bytes 1966088 | tf_op jit(solution)/shard_map/ppermute | solution.py:70
  244.2 3.8 copy-start.1
  244.3 13.1 %collective-permute-start.20 = (bf16[640,256]{1,0:T(8,128)(2,1)S(1)}, bf16[640,256]{1,0:T(8,128)(2,1)S(1)}, u32[]{:S(2)}, u32[]{:S(2)}) collective-permute-start(bf16[640,256]{1,0:T(8,128)(2,1)S(1)} %add_convert_fusion.4), channel_id=1, source_target_pairs={{8,0},{12,4},{9,1},{13,5},{10,2},{14,6},{11,3},{15,7},{24,16},{28,... | collective-permute-start | bytes 983048 | tf_op jit(solution)/shard_map/ppermute | solution.py:348
  245.6 11.8 %copy-start.2 = (bf16[960,896]{0,1:T(8,128)(2,1)}, bf16[960,896]{0,1:T(8,128)(2,1)S(1)}, u32[]{:S(2)}) copy-start(bf16[960,896]{0,1:T(8,128)(2,1)S(1)} %broadcast_dynamic-update-slice_fusion) | copy-start | bytes 5160964
  247.9 11.1 %copy-start.13 = (bf16[960,384]{1,0:T(8,128)(2,1)S(1)}, bf16[960,384]{1,0:T(8,128)(2,1)}, u32[]{:S(2)}) copy-start(bf16[960,384]{1,0:T(8,128)(2,1)} %get-tuple-element.140) | copy-start | bytes 2211844
  248.0 11.1 %copy-start.14 = (bf16[960,384]{1,0:T(8,128)(2,1)S(1)}, bf16[960,384]{1,0:T(8,128)(2,1)}, u32[]{:S(2)}) copy-start(bf16[960,384]{1,0:T(8,128)(2,1)} %get-tuple-element.138) | copy-start | bytes 2211844
  248.0 11.1 %copy-start.15 = (bf16[960,384]{1,0:T(8,128)(2,1)S(1)}, bf16[960,384]{1,0:T(8,128)(2,1)}, u32[]{:S(2)}) copy-start(bf16[960,384]{1,0:T(8,128)(2,1)} %get-tuple-element.136) | copy-start | bytes 2211844
  262.8 31.8 %all-to-all-start.3 = ((bf16[8,120,1152]{2,1,0:T(8,128)(2,1)}), bf16[8,120,1152]{2,1,0:T(8,128)(2,1)}, u32[]{:S(2)}, u32[]{:S(2)}) async-start(bf16[8,120,1152]{2,1,0:T(8,128)(2,1)} %bitcast.60), calls=%async_computation.3 | async-start | bytes 4423680 | tf_op jit(solution)/shard_map/all_to_all | solution.py:52
  267.2 4.8 %copy-start.3 = (bf16[960,896]{0,1:T(8,128)(2,1)S(1)}, bf16[960,896]{0,1:T(8,128)(2,1)}, u32[]{:S(2)}) copy-start(bf16[960,896]{0,1:T(8,128)(2,1)} %copy-done.2) | copy-start | bytes 5160964
  275.4 4.9 %copy-start.37 = (pred[512]{0:T(512)(128)(4,1)S(1)}, pred[512]{0:T(512)(128)(4,1)}, u32[]{:S(2)}) copy-start(pred[512]{0:T(512)(128)(4,1)} %constant.38.clone.1) | copy-start | bytes 1540
  279.2 20.7 %collective-permute-start.21 = (bf16[960,896]{1,0:T(8,128)(2,1)}, bf16[960,896]{1,0:T(8,128)(2,1)}, u32[]{:S(2)}, u32[]{:S(2)}) collective-permute-start(bf16[960,896]{1,0:T(8,128)(2,1)} %copy.95), channel_id=1, source_target_pairs={{0,4},{4,0},{8,12},{12,8},{1,5},{5,1},{9,13},{13,9},{2,6},{6,2},{1... | collective-permute-start | bytes 5160968 | tf_op jit(solution)/shard_map/ppermute | solution.py:70
  283.1 13.6 %collective-permute-start.22 = (bf16[960,512]{1,0:T(8,128)(2,1)}, bf16[960,512]{1,0:T(8,128)(2,1)}, u32[]{:S(2)}, u32[]{:S(2)}) collective-permute-start(bf16[960,512]{1,0:T(8,128)(2,1)} %broadcast_select_fusion.4), channel_id=1, source_target_pairs={{0,4},{4,0},{8,12},{12,8},{1,5},{5,1},{9,13},{13,9},{2,6},{6,2},{1... | collective-permute-start | bytes 2949128 | tf_op jit(solution)/shard_map/ppermute | solution.py:70
  296.6 11.3 %collective-permute-start.32 = (bf16[120,1152]{1,0:T(8,128)(2,1)S(1)}, bf16[120,1152]{1,0:T(8,128)(2,1)}, u32[]{:S(2)}, u32[]{:S(2)}) collective-permute-start(bf16[120,1152]{1,0:T(8,128)(2,1)S(1)} %reduce_sum.106), channel_id=1, source_target_pairs={{0,8},{4,12},{8,0},{12,4},{1,9},{5,13},{9,1},{13,5},{2,10},{6,14},... | collective-permute-start | bytes 829448 | tf_op jit(solution)/shard_map/ppermute | solution.py:377
  303.6 18.5 %all-to-all-start.4 = ((bf16[8,120,512]{2,1,0:T(8,128)(2,1)}), bf16[8,120,512]{2,1,0:T(8,128)(2,1)}, u32[]{:S(2)}, u32[]{:S(2)}) async-start(bf16[8,120,512]{2,1,0:T(8,128)(2,1)} %bitcast.65), calls=%async_computation.4 | async-start | bytes 1966080 | tf_op jit(solution)/shard_map/all_to_all | solution.py:52
  309.7 24.2 %collective-permute-start.33 = (f32[120,1152]{1,0:T(8,128)}, f32[120,1152]{1,0:T(8,128)}, u32[]{:S(2)}, u32[]{:S(2)}) collective-permute-start(f32[120,1152]{1,0:T(8,128)} %convert_add_fusion.1), channel_id=1, source_target_pairs={{0,4},{4,0},{8,12},{12,8},{1,5},{5,1},{9,13},{13,9},{2,6},{6,2},{1... | collective-permute-start | bytes 1658888 | tf_op jit(solution)/shard_map/ppermute | solution.py:70
  327.9 25.8 %all-to-all-start.5 = ((bf16[8,120,896]{2,1,0:T(8,128)(2,1)}), bf16[8,120,896]{2,1,0:T(8,128)(2,1)S(1)}, u32[]{:S(2)}, u32[]{:S(2)}) async-start(bf16[8,120,896]{2,1,0:T(8,128)(2,1)} %bitcast.63), calls=%async_computation.5 | async-start | bytes 3440640 | tf_op jit(solution)/shard_map/all_to_all | solution.py:52
  335.3 18.8 %collective-permute-start.28 = (bf16[120,512]{1,0:T(8,128)(2,1)S(1)}, bf16[120,512]{1,0:T(8,128)(2,1)S(1)}, u32[]{:S(2)}, u32[]{:S(2)}) collective-permute-start(bf16[120,512]{1,0:T(8,128)(2,1)S(1)} %copy-done.25), channel_id=1, source_target_pairs={{0,1},{1,0},{2,3},{3,2},{4,5},{5,4},{6,7},{7,6},{8,9},{9,8},{10,11... | collective-permute-start | bytes 368648 | tf_op jit(solution)/shard_map/ppermute | solution.py:381
  353.9 6.1 %collective-permute-start.24 = (bf16[120,896]{1,0:T(8,128)(2,1)S(1)}, bf16[120,896]{1,0:T(8,128)(2,1)S(1)}, u32[]{:S(2)}, u32[]{:S(2)}) collective-permute-start(bf16[120,896]{1,0:T(8,128)(2,1)S(1)} %reduce_sum.108), channel_id=1, source_target_pairs={{0,1},{1,0},{2,3},{3,2},{4,5},{5,4},{6,7},{7,6},{8,9},{9,8},{10,11... | collective-permute-start | bytes 645128 | tf_op jit(solution)/shard_map/ppermute | solution.py:381
  354.1 6.2 %collective-permute-start.29 = (bf16[120,512]{1,0:T(8,128)(2,1)S(1)}, bf16[120,512]{1,0:T(8,128)(2,1)S(1)}, u32[]{:S(2)}, u32[]{:S(2)}) collective-permute-start(bf16[120,512]{1,0:T(8,128)(2,1)S(1)} %add_convert_fusion.9), channel_id=1, source_target_pairs={{0,3},{3,0},{1,2},{2,1},{4,7},{7,4},{5,6},{6,5},{8,11},{11,8},{9,1... | collective-permute-start | bytes 368648 | tf_op jit(solution)/shard_map/ppermute | solution.py:381
  360.2 6.5 %collective-permute-start.25 = (bf16[120,896]{1,0:T(8,128)(2,1)S(1)}, bf16[120,896]{1,0:T(8,128)(2,1)S(1)}, u32[]{:S(2)}, u32[]{:S(2)}) collective-permute-start(bf16[120,896]{1,0:T(8,128)(2,1)S(1)} %add_convert_fusion.6), channel_id=1, source_target_pairs={{0,3},{3,0},{1,2},{2,1},{4,7},{7,4},{5,6},{6,5},{8,11},{11,8},{9,1... | collective-permute-start | bytes 645128 | tf_op jit(solution)/shard_map/ppermute | solution.py:381
  360.3 9.6 %collective-permute-start.30 = (bf16[120,512]{1,0:T(8,128)(2,1)S(1)}, bf16[120,512]{1,0:T(8,128)(2,1)S(1)}, u32[]{:S(2)}, u32[]{:S(2)}) collective-permute-start(bf16[120,512]{1,0:T(8,128)(2,1)S(1)} %add_convert_fusion.8), channel_id=1, source_target_pairs={{0,8},{4,12},{8,0},{12,4},{1,9},{5,13},{9,1},{13,5},{2,10},{6,14},... | collective-permute-start | bytes 368648 | tf_op jit(solution)/shard_map/ppermute | solution.py:377
  366.7 6.4 %collective-permute-start.26 = (bf16[120,896]{1,0:T(8,128)(2,1)S(1)}, bf16[120,896]{1,0:T(8,128)(2,1)S(1)}, u32[]{:S(2)}, u32[]{:S(2)}) collective-permute-start(bf16[120,896]{1,0:T(8,128)(2,1)S(1)} %add_convert_fusion.5), channel_id=1, source_target_pairs={{0,8},{4,12},{8,0},{12,4},{1,9},{5,13},{9,1},{13,5},{2,10},{6,14},... | collective-permute-start | bytes 645128 | tf_op jit(solution)/shard_map/ppermute | solution.py:377
  369.9 7.8 %collective-permute-start.31 = (f32[120,512]{1,0:T(8,128)S(1)}, f32[120,512]{1,0:T(8,128)S(1)}, u32[]{:S(2)}, u32[]{:S(2)}) collective-permute-start(f32[120,512]{1,0:T(8,128)S(1)} %convert_add_fusion.3), channel_id=1, source_target_pairs={{0,4},{4,0},{8,12},{12,8},{1,5},{5,1},{9,13},{13,9},{2,6},{6,2},{1... | collective-permute-start | bytes 737288 | tf_op jit(solution)/shard_map/ppermute | solution.py:70
  373.2 5.5 %collective-permute-start.27 = (f32[120,896]{1,0:T(8,128)S(1)}, f32[120,896]{1,0:T(8,128)S(1)}, u32[]{:S(2)}, u32[]{:S(2)}) collective-permute-start(f32[120,896]{1,0:T(8,128)S(1)} %convert_add_fusion.2), channel_id=1, source_target_pairs={{0,4},{4,0},{8,12},{12,8},{1,5},{5,1},{9,13},{13,9},{2,6},{6,2},{1... | collective-permute-start | bytes 1290248 | tf_op jit(solution)/shard_map/ppermute | solution.py:70
  (14 other events, 23.0 us)
